TPU v7x, 256 devices: a whole 4x4x8 slice. The times are simulated.
256 devices in a mesh: dp: 2 (over core), expert: 128 (over z, x, y).
Axes of the slice: x: 4, y: 4, z: 8, core: 2. Of those that a mesh axis runs over, the one named last changes fastest.
Arguments:
- tokens: bfloat16 [32768, 2048], P(('dp', 'expert')), may hold values from -6 to 6
- out_grad: bfloat16 [32768, 2048], P(('dp', 'expert')), may hold values from -6 to 6
- expert_ids: int32 [32768, 4], P(('dp', 'expert')), may hold values from 0 to 127, as said below
- gate_weights: float32 [32768, 4], P(('dp', 'expert')), may hold values from 0.05 to 0.6
- w_in: bfloat16 [128, 2048, 768], P('expert'), may hold values from -0.125 to 0.125
- w_out: bfloat16 [128, 384, 2048], P('expert'), may hold values from -0.3125 to 0.3125
Outputs:
- token_grad: bfloat16 [32768, 2048], P(('dp', 'expert'))
- w_in_grad: bfloat16 [128, 2048, 768], P('expert', 'dp')
- w_out_grad: bfloat16 [128, 384, 2048], P('expert', None, 'dp')
Inputs may be any that keep to these rules, and one draw needn't show every extreme that they name: `expert_ids`: each token names 4 different experts; among the 128 tokens of one device no expert is named more than 7 times, and in every device's tokens some expert is named exactly 7 times.
All inputs are finite; a program needn't handle non-finite values.
Results may differ from a plain program's by a relative error of at most 0.0065.
Values may be sent and summed in bfloat16 or wider, within the bound.
No kernel may reach another device: no remote copies, remote signals or barrier semaphores. Data moves between devices by JAX's collectives and lax.ppermute only.
A program may use at most 128 MiB of HBM per device.

v0:
```python
import jax
import jax.numpy as jnp
from jax import lax
from jax.sharding import PartitionSpec as P


def partner(x, axis, distance):
    return lax.ppermute(x, axis, [(i, i ^ 1 << distance) for i in range(lax.axis_size(axis))])


def silu_parts(gate_part):
    sigma = 1.0 / (1.0 + jnp.exp(-gate_part))
    return (gate_part * sigma, sigma * (1.0 + gate_part * (1.0 - sigma)))


def backward_rows(rows_in, rows_grad, weight_in, weight_out):
    hidden_width = weight_out.shape[0]
    joined = jnp.dot(rows_in, weight_in, preferred_element_type=jnp.float32)
    gate_part = joined[:, :hidden_width]
    up_part = joined[:, hidden_width:]
    activated, derivative = silu_parts(gate_part)
    hidden = (activated * up_part).astype(jnp.bfloat16)
    d_hidden = lax.dot_general(
        rows_grad, weight_out, (((1,), (1,)), ((), ())), preferred_element_type=jnp.float32
    )
    d_joined = jnp.concatenate(
        [d_hidden * up_part * derivative, d_hidden * activated], axis=1
    ).astype(jnp.bfloat16)
    d_rows = lax.dot_general(
        d_joined, weight_in, (((1,), (1,)), ((), ())), preferred_element_type=jnp.float32
    ).astype(jnp.bfloat16)
    grad_in = lax.dot_general(
        rows_in, d_joined, (((0,), (0,)), ((), ())), preferred_element_type=jnp.float32
    )
    grad_out = lax.dot_general(
        hidden, rows_grad, (((0,), (0,)), ((), ())), preferred_element_type=jnp.float32
    )
    return (d_rows, grad_in, grad_out)


def body(tokens, out_grad, expert_ids, gate_weights, w_in, w_out):
    hosts = lax.axis_size("expert")
    half_axis = hosts // 2
    swap_bit = hosts.bit_length() - 2
    token_count = tokens.shape[0]
    model_width = tokens.shape[1]
    route_width = expert_ids.shape[1]
    capacity = max(2, 7 * token_count * route_width // (4 * hosts))
    spare_slots = max(1, capacity // 3)
    primary_slots = capacity - spare_slots
    route_ids = expert_ids.reshape(-1)
    total_routes = route_ids.shape[0]
    route_tok = jnp.arange(total_routes, dtype=jnp.int32) // route_width
    onehot = (route_ids[:, None] == jnp.arange(hosts, dtype=jnp.int32)[None, :]).astype(jnp.int32)
    before = jnp.cumsum(onehot, axis=0) - onehot
    slot_rank = jnp.sum(before * onehot, axis=1)
    target = jnp.where(slot_rank < primary_slots, route_ids, (route_ids + half_axis) % hosts)
    position = target * capacity + slot_rank
    filled = (
        jnp.zeros((hosts * capacity,), jnp.int32)
        .at[position]
        .set(jnp.arange(total_routes, dtype=jnp.int32) + 1)
    )
    occupied = filled > 0
    source = jnp.maximum(filled - 1, 0)
    scaled = (gate_weights.reshape(-1)[:, None] * out_grad[route_tok].astype(jnp.float32)).astype(
        jnp.bfloat16
    )
    zero_value = jnp.zeros((), jnp.bfloat16)
    send_in = jnp.where(occupied[:, None], tokens[route_tok[source]], zero_value)
    send_grad = jnp.where(occupied[:, None], scaled[source], zero_value)
    got_in, got_grad = (
        lax.all_to_all(send_in, "expert", split_axis=0, concat_axis=0, tiled=True),
        lax.all_to_all(send_grad, "expert", split_axis=0, concat_axis=0, tiled=True),
    )
    own_in = w_in[0]
    own_out = w_out[0]
    copy_in, copy_out = partner((own_in, own_out), "expert", swap_bit)
    blocks_in = got_in.reshape(hosts, capacity, model_width)
    blocks_grad = got_grad.reshape(hosts, capacity, model_width)
    d_own, gin_own, gout_own = backward_rows(
        blocks_in[:, :primary_slots].reshape(-1, model_width),
        blocks_grad[:, :primary_slots].reshape(-1, model_width),
        own_in,
        own_out,
    )
    d_copy, gin_copy, gout_copy = backward_rows(
        blocks_in[:, primary_slots:].reshape(-1, model_width),
        blocks_grad[:, primary_slots:].reshape(-1, model_width),
        copy_in,
        copy_out,
    )
    d_slots = jnp.concatenate(
        [
            d_own.reshape(hosts, primary_slots, model_width),
            d_copy.reshape(hosts, spare_slots, model_width),
        ],
        axis=1,
    )
    d_slots = d_slots.reshape(hosts * capacity, model_width)
    back_in, back_out = (
        partner(gin_copy.astype(jnp.bfloat16), "expert", swap_bit).astype(gin_copy.dtype),
        partner(gout_copy.astype(jnp.bfloat16), "expert", swap_bit).astype(gout_copy.dtype),
    )
    sum_in, sum_out = (
        lax.psum_scatter(gin_own + back_in, "dp", scatter_dimension=0, tiled=True),
        lax.psum_scatter(gout_own + back_out, "dp", scatter_dimension=1, tiled=True),
    )
    returned = lax.all_to_all(d_slots, "expert", split_axis=0, concat_axis=0, tiled=True)
    per_route = returned[position].reshape(token_count, route_width, model_width)
    token_grad = jnp.sum(per_route.astype(jnp.float32), axis=1).astype(jnp.bfloat16)
    return (token_grad, sum_in.astype(jnp.bfloat16)[None], sum_out.astype(jnp.bfloat16)[None])


def solution(mesh):
    in_specs = (
        P(("dp", "expert"), None),
        P(("dp", "expert"), None),
        P(("dp", "expert"), None),
        P(("dp", "expert"), None),
        P("expert", None, None),
        P("expert", None, None),
    )
    out_specs = (P(("dp", "expert"), None), P("expert", "dp", None), P("expert", None, "dp"))
    return jax.shard_map(body, mesh=mesh, in_specs=in_specs, out_specs=out_specs, check_vma=False)
```

profile of v0, /device:TPU:1, one launch (start us, length us, event | category | flops | bytes accessed | tf_op | source)
XLA Modules:
  0.0 847.9 jit_solution(15367783464398113201)
XLA Ops:
  7.2 0.0 copy-start
  7.2 0.8 copy.11
  8.1 0.1 reshape.203
  8.2 0.0 copy-start.2
  8.2 0.1 eq.31
  8.3 0.1 eq.27
  8.4 0.1 copy.13
  8.5 0.2 fusion.6
  8.8 0.2 fusion.5
  9.1 2.4 scatter_custom_fusion
  11.6 0.8 copy.16
  12.4 0.1 mul.71
  12.5 5.8 gather_fusion.2
  18.3 0.2 broadcast_in_dim.35
  18.6 3.3 gather_fusion
  21.9 2.0 multiply_convert_fusion
  23.9 5.0 gather_fusion.1
  28.9 6.1 gather.23
  35.0 5.0 gather_fusion.3
  40.0 6.0 gather.27
  46.0 5.1 broadcast_select_fusion
  51.1 109.9 %all_to_all.21 = bf16[128,7,2048]{2,1,0:T(8,128)(2,1)} all-to-all(bf16[128,7,2048]{2,1,0:T(8,128)(2,1)S(1)} %get-tuple-element.8), channel_id=1, replica_groups=mesh['dp'=2,'expert'=128] {'expert'}, dimensions={0} | all-to-all | bytes 7340032 | tf_op jit(solution)/shard_map/all_to_all | solution.py:74
  161.0 11.3 %all-to-all-start.1 = ((bf16[128,7,2048]{2,1,0:T(8,128)(2,1)}), bf16[128,7,2048]{2,1,0:T(8,128)(2,1)}, u32[]{:S(2)}, u32[]{:S(2)}) async-start(bf16[128,7,2048]{2,1,0:T(8,128)(2,1)} %get-tuple-element.7), calls=%async_computation.1 | async-start | bytes 8388608 | tf_op jit(solution)/shard_map/all_to_all | solution.py:73
  172.4 0.0 reduce-scatter.5.cloned.1.call-start
  172.4 5.3 collective-permute-start.1
  177.7 3.3 slice.55
  181.0 1.2 reshape.207
  182.3 82.6 %all-to-all-done.1 = bf16[128,7,2048]{2,1,0:T(8,128)(2,1)} async-done(((bf16[128,7,2048]{2,1,0:T(8,128)(2,1)}), bf16[128,7,2048]{2,1,0:T(8,128)(2,1)}, u32[]{:S(2)}, u32[]{:S(2)}) %all-to-all-start.1) | async-done | bytes 3670048 | tf_op jit(solution)/shard_map/all_to_all | solution.py:73
  264.9 3.3 slice.56
  268.2 0.4 reshape.208
  268.7 0.0 copy-start.6
  268.7 113.3 %collective-permute-done.1 = bf16[2048,768]{1,0:T(8,128)(2,1)} collective-permute-done((bf16[2048,768]{1,0:T(8,128)(2,1)}, bf16[2048,768]{1,0:T(8,128)(2,1)}, u32[]{:S(2)}, u32[]{:S(2)}) %collective-permute-start.1) | collective-permute-done | bytes 3145760 | tf_op jit(solution)/shard_map/ppermute | solution.py:8
  382.0 2.9 fusion.29
  384.9 1.8 convolution_convert_fusion.2
  386.7 5.6 reshape.204
  392.3 5.6 reshape.205
  397.9 5.6 fusion.23
  403.5 20.5 %collective-permute-done.3 = bf16[384,2048]{1,0:T(8,128)(2,1)} collective-permute-done((bf16[384,2048]{1,0:T(8,128)(2,1)}, bf16[384,2048]{1,0:T(8,128)(2,1)}, u32[]{:S(2)}, u32[]{:S(2)}) %collective-permute-start.3) | collective-permute-done | bytes 1572896 | tf_op jit(solution)/shard_map/ppermute | solution.py:8
  424.0 4.5 convert_add_fusion.1
  428.5 0.0 reduce-scatter.5.cloned.1.call-update
  428.5 0.0 reduce-scatter.3.cloned.1.call-start
  428.6 6.2 collective-permute-start
  434.8 60.3 %collective-permute-done = bf16[384,2048]{1,0:T(8,128)(2,1)S(1)} collective-permute-done((bf16[384,2048]{1,0:T(8,128)(2,1)}, bf16[384,2048]{1,0:T(8,128)(2,1)S(1)}, u32[]{:S(2)}, u32[]{:S(2)}) %collective-permute-start) | collective-permute-done | bytes 1572896 | tf_op jit(solution)/shard_map/ppermute | solution.py:8
  495.1 0.8 multiply_convert_fusion.9
  495.9 0.0 copy-start.7
  495.9 1.0 convolution_convert_fusion
  496.9 6.4 collective-permute-start.2
  503.3 1.6 multiply_convert_fusion.3
  505.0 58.6 %collective-permute-done.2 = bf16[2048,768]{1,0:T(8,128)(2,1)S(1)} collective-permute-done((bf16[2048,768]{1,0:T(8,128)(2,1)S(1)}, bf16[2048,768]{1,0:T(8,128)(2,1)S(1)}, u32[]{:S(2)}, u32[]{:S(2)}) %collective-permute-start.2) | collective-permute-done | bytes 3145760 | tf_op jit(solution)/shard_map/ppermute | solution.py:8
  563.6 4.6 convert_add_fusion
  568.2 0.0 reduce-scatter.3.cloned.1.call-update
  568.2 2.9 convolution_convert_fusion.3
  571.1 0.7 reshape.209
  571.9 5.8 convolution_convert_fusion.1
  577.6 5.5 reshape.206
  583.1 5.3 pad_maximum_fusion
  588.4 135.7 %all-to-all-start.2 = ((bf16[128,7,2048]{2,1,0:T(8,128)(2,1)}), bf16[128,7,2048]{2,1,0:T(8,128)(2,1)}, u32[]{:S(2)}, u32[]{:S(2)}) async-start(bf16[128,7,2048]{2,1,0:T(8,128)(2,1)} %pad_maximum_fusion), calls=%async_computation.2 | async-start | bytes 8388608 | tf_op jit(solution)/shard_map/all_to_all | solution.py:109
  724.1 90.9 %all-to-all-done.2 = bf16[128,7,2048]{2,1,0:T(8,128)(2,1)} async-done(((bf16[128,7,2048]{2,1,0:T(8,128)(2,1)}), bf16[128,7,2048]{2,1,0:T(8,128)(2,1)}, u32[]{:S(2)}, u32[]{:S(2)}) %all-to-all-start.2) | async-done | bytes 3670048 | tf_op jit(solution)/shard_map/all_to_all | solution.py:109
  815.0 6.1 all_to_all.17
  821.1 6.9 gather_fusion.4
  828.0 2.2 reshape.210
  830.2 5.0 reduce_sum.25
  835.2 2.4 convert_bitcast_fusion.1
  837.6 3.2 convert_bitcast_fusion
  (38 shorter events, 0.2 us)
Async XLA Ops:
  7.2 27.8 %copy-start = (bf16[128,2048]{1,0:T(8,128)(2,1)S(1)}, bf16[128,2048]{1,0:T(8,128)(2,1)}, u32[]{:S(2)}) copy-start(bf16[128,2048]{1,0:T(8,128)(2,1)} %param.6) | copy-start | bytes 1572868
  8.2 10.4 %copy-start.2 = (bf16[128,2048]{1,0:T(8,128)(2,1)S(1)}, bf16[128,2048]{1,0:T(8,128)(2,1)}, u32[]{:S(2)}) copy-start(bf16[128,2048]{1,0:T(8,128)(2,1)} %param.7) | copy-start | bytes 1572868
  161.0 103.8 %all-to-all-start.1 = ((bf16[128,7,2048]{2,1,0:T(8,128)(2,1)}), bf16[128,7,2048]{2,1,0:T(8,128)(2,1)}, u32[]{:S(2)}, u32[]{:S(2)}) async-start(bf16[128,7,2048]{2,1,0:T(8,128)(2,1)} %get-tuple-element.7), calls=%async_computation.1 | async-start | bytes 8388608 | tf_op jit(solution)/shard_map/all_to_all | solution.py:73
  172.4 662.8 %reduce-scatter.5.cloned.1.call-start = ((), (), s32[]{:S(2)}) async-start(), calls=%async_computation.6 | async-start | bytes 4718592 | tf_op jit(solution)/shard_map/reduce_scatter | solution.py:107
  172.4 209.6 %collective-permute-start.1 = (bf16[2048,768]{1,0:T(8,128)(2,1)}, bf16[2048,768]{1,0:T(8,128)(2,1)}, u32[]{:S(2)}, u32[]{:S(2)}) collective-permute-start(bf16[2048,768]{1,0:T(8,128)(2,1)} %bitcast.52), channel_id=1, source_target_pairs={{0,64},{1,65},{2,66},{3,67},{4,68},{5,69},{6,70},{7,71},{8,72},{9,... | collective-permute-start | bytes 9437192 | tf_op jit(solution)/shard_map/ppermute | solution.py:8
  268.7 116.2 %copy-start.6 = (bf16[256,2048]{1,0:T(8,128)(2,1)S(1)}, bf16[256,2048]{1,0:T(8,128)(2,1)}, u32[]{:S(2)}) copy-start(bf16[256,2048]{1,0:T(8,128)(2,1)} %reshape.207) | copy-start | bytes 3145732
  386.7 37.3 %collective-permute-start.3 = (bf16[384,2048]{1,0:T(8,128)(2,1)}, bf16[384,2048]{1,0:T(8,128)(2,1)}, u32[]{:S(2)}, u32[]{:S(2)}) collective-permute-start(bf16[384,2048]{1,0:T(8,128)(2,1)} %convolution_convert_fusion.2), channel_id=1, source_target_pairs={{0,64},{1,65},{2,66},{3,67},{4,68},{5,69},{6,70},{7,71},{8,72},{9,... | collective-permute-start | bytes 4718600 | tf_op jit(solution)/shard_map/ppermute | solution.py:8
  397.9 26.1 %copy-start.4 = (bf16[640,2048]{1,0:T(8,128)(2,1)S(1)}, bf16[640,2048]{1,0:T(8,128)(2,1)}, u32[]{:S(2)}) copy-start(bf16[640,2048]{1,0:T(8,128)(2,1)} %reshape.204) | copy-start | bytes 7864324
  403.5 20.5 %copy-start.8 = (f32[640,768]{0,1:T(8,128)}, f32[640,768]{0,1:T(8,128)S(1)}, u32[]{:S(2)}) copy-start(f32[640,768]{0,1:T(8,128)S(1)} %fusion.23) | copy-start | bytes 5898244
  428.5 409.1 %reduce-scatter.3.cloned.1.call-start = ((), (), s32[]{:S(2)}) async-start(), calls=%async_computation.5 | async-start | bytes 9437184 | tf_op jit(solution)/shard_map/reduce_scatter | solution.py:106
  428.6 66.5 %collective-permute-start = (bf16[384,2048]{1,0:T(8,128)(2,1)}, bf16[384,2048]{1,0:T(8,128)(2,1)S(1)}, u32[]{:S(2)}, u32[]{:S(2)}) collective-permute-start(bf16[384,2048]{1,0:T(8,128)(2,1)} %bitcast.53), channel_id=1, source_target_pairs={{0,64},{1,65},{2,66},{3,67},{4,68},{5,69},{6,70},{7,71},{8,72},{9,... | collective-permute-start | bytes 4718600 | tf_op jit(solution)/shard_map/ppermute | solution.py:8
  495.8 7.5 copy-start.5
  495.9 7.5 copy-start.7
  495.9 7.5 copy-start.9
  496.9 66.6 %copy-start.3 = (bf16[640,2048]{1,0:T(8,128)(2,1)S(1)}, bf16[640,2048]{1,0:T(8,128)(2,1)}, u32[]{:S(2)}) copy-start(bf16[640,2048]{1,0:T(8,128)(2,1)} %reshape.205) | copy-start | bytes 7864324
  496.9 66.6 %collective-permute-start.2 = (bf16[2048,768]{1,0:T(8,128)(2,1)S(1)}, bf16[2048,768]{1,0:T(8,128)(2,1)S(1)}, u32[]{:S(2)}, u32[]{:S(2)}) collective-permute-start(bf16[2048,768]{1,0:T(8,128)(2,1)S(1)} %convolution_convert_fusion), channel_id=1, source_target_pairs={{0,64},{1,65},{2,66},{3,67},{4,68},{5,69},{6,70},{7,71},{8,72},{9,... | collective-permute-start | bytes 9437192 | tf_op jit(solution)/shard_map/ppermute | solution.py:8
  504.9 58.6 %copy-start.10 = (bf16[640,384]{0,1:T(8,128)(2,1)}, bf16[640,384]{0,1:T(8,128)(2,1)S(1)}, u32[]{:S(2)}) copy-start(bf16[640,384]{0,1:T(8,128)(2,1)S(1)} %get-tuple-element.4) | copy-start | bytes 1474564
  588.4 226.6 %all-to-all-start.2 = ((bf16[128,7,2048]{2,1,0:T(8,128)(2,1)}), bf16[128,7,2048]{2,1,0:T(8,128)(2,1)}, u32[]{:S(2)}, u32[]{:S(2)}) async-start(bf16[128,7,2048]{2,1,0:T(8,128)(2,1)} %pad_maximum_fusion), calls=%async_computation.2 | async-start | bytes 8388608 | tf_op jit(solution)/shard_map/all_to_all | solution.py:109
  830.2 10.6 %copy-start.1 = (bf16[128,2048]{1,0:T(8,128)(2,1)S(1)}, bf16[128,2048]{1,0:T(8,128)(2,1)}, u32[]{:S(2)}) copy-start(bf16[128,2048]{1,0:T(8,128)(2,1)} %param.6) | copy-start | bytes 1572868
Sparse Core Ops, SparseCore 0:
  428.6 159.6 reduce-scatter.4
  591.1 121.2 reduce-scatter.2
where the time goes:
time: 861 us; the launch traced here: 848 us
  waiting for transfers between devices  426 us (49%)
  starting transfers between devices  165 us (19%)
  blocking collectives  110 us (13%)
  local copies, waits for them, and re-layouts  77.1 us (9%)
  matrix products  31.4 us (4%)
  other arithmetic  23.6 us (3%)
  between operations  14.6 us (2%)
    ppermute x4, waiting for transfers between devices, partner(): lax.ppermute(x, axis, [(i, i ^ 1 << distance) for i in range(lax.axis_siz...  253 us
    all_to_all x1, starting transfers between devices, body(): lax.all_to_all(d_slots, 'expert', split_axis=0, concat_axis=0, tiled=True)  136 us
    all_to_all x1, blocking collectives, body(): lax.all_to_all(send_grad, 'expert', split_axis=0, concat_axis=0, tiled=True)  110 us
    all_to_all x1, waiting for transfers between devices, body(): lax.all_to_all(d_slots, 'expert', split_axis=0, concat_axis=0, tiled=True)  90.9 us
    all_to_all x1, waiting for transfers between devices, body(): lax.all_to_all(send_in, 'expert', split_axis=0, concat_axis=0, tiled=True)  82.6 us
    ppermute x4, starting transfers between devices, partner(): lax.ppermute(x, axis, [(i, i ^ 1 << distance) for i in range(lax.axis_siz...  17.9 us
  transfers between devices with their start and end apart: 8, of which 6 were waited for; matrix products, arithmetic and copies ran while one was open for 8% of the time, Pallas kernels for 0%

commit v1 on v0

v1 whole, which is shorter than its diff:
```python
import jax
import jax.numpy as jnp
from jax import lax
from jax.sharding import Mesh
from jax.sharding import PartitionSpec as P

Z, X, Y = 8, 4, 4
PLANE = X * Y
CAP = 7
IN_CHUNKS = 1
GRAD_CHUNKS = 1
BACK_CHUNKS = 1

f32 = jnp.float32
bf16 = jnp.bfloat16


def mm(a, b, ca, cb):
    return lax.dot_general(a, b, (((ca,), (cb,)), ((), ())), preferred_element_type=f32)


def pieces(width, count):
    step = width // count
    return [(i * step, (i + 1) * step) for i in range(count)]


def silu_parts(gate_part):
    sigma = 1.0 / (1.0 + jnp.exp(-gate_part))
    return gate_part * sigma, sigma * (1.0 + gate_part * (1.0 - sigma))


def routing(meta, plane):
    sources, tok = Z, meta.shape[-1]
    meta = meta.reshape(sources, 8, tok)
    ids = meta[:, :4].astype(jnp.int32)
    gates = meta[:, 4:]
    local = plane * PLANE + jnp.arange(PLANE, dtype=jnp.int32)
    match = ids[:, :, None, :] == local[None, None, :, None]
    named = jnp.any(match, axis=1)
    gate = jnp.sum(jnp.where(match, gates[:, :, None, :], 0.0), axis=1)
    index = jnp.arange(tok, dtype=jnp.int32)
    earlier = (index[:, None] < index[None, :]).astype(bf16)
    before = mm(named.astype(bf16).reshape(sources * PLANE, tok), earlier, 1, 0)
    rank = jnp.where(named, before.reshape(sources, PLANE, tok), -1.0)
    rank = rank.transpose(1, 0, 2)
    gate = gate.transpose(1, 0, 2)
    slot_rank = jnp.arange(CAP, dtype=jnp.int32).astype(f32)
    hit = rank[:, None] == slot_rank[None, :, None, None]
    slot_gate = jnp.sum(jnp.where(hit, gate[:, None], 0.0), axis=3).reshape(-1, 1)
    same = jnp.arange(sources)[:, None] == jnp.arange(sources)[None, :]
    wide = jnp.where(same[None, :, :, None], rank[:, None], -1.0).reshape(PLANE, 1, sources, sources * tok)
    slots = (wide == slot_rank[None, :, None, None]).astype(bf16)
    return slots.reshape(PLANE * CAP * sources, sources * tok), slot_gate


def body(tokens, out_grad, expert_ids, gate_weights, w_in, w_out):
    width = tokens.shape[1]
    w_in, w_out = w_in[0], w_out[0]
    half = w_out.shape[0]
    plane = lax.axis_index("z")
    core = lax.axis_index("dp")

    def gather_z(x):
        return lax.all_gather(x, "z", axis=0, tiled=True)

    def swap_plane(x):
        return lax.all_to_all(x, ("x", "y"), split_axis=0, concat_axis=0, tiled=True)

    meta = gather_z(jnp.concatenate([expert_ids.astype(f32), gate_weights], axis=1).T)
    slots, slot_gate = routing(meta, plane)

    rows_in = []
    for lo, hi in pieces(width, IN_CHUNKS):
        every = gather_z(tokens[:, lo:hi])
        rows_in.append(swap_plane(mm(slots, every, 1, 0).astype(bf16)))
    rows_grad = []
    for lo, hi in pieces(width, GRAD_CHUNKS):
        every = gather_z(out_grad[:, lo:hi])
        rows_grad.append(swap_plane((mm(slots, every, 1, 0) * slot_gate).astype(bf16)))

    joined = sum(mm(r, w_in[lo:hi], 1, 0) for r, (lo, hi) in zip(rows_in, pieces(width, IN_CHUNKS)))
    d_hidden = sum(mm(r, w_out[:, lo:hi], 1, 1) for r, (lo, hi) in zip(rows_grad, pieces(width, GRAD_CHUNKS)))
    gate_part, up_part = joined[:, :half], joined[:, half:]
    activated, derivative = silu_parts(gate_part)
    hidden = (activated * up_part).astype(bf16)
    d_joined = jnp.concatenate([d_hidden * up_part * derivative, d_hidden * activated], axis=1).astype(bf16)

    token_grad = []
    for lo, hi in pieces(width, BACK_CHUNKS):
        back = swap_plane(mm(d_joined, w_in[lo:hi], 1, 1).astype(bf16))
        part = mm(slots, back, 0, 0).astype(bf16)
        token_grad.append(lax.psum_scatter(part, "z", scatter_dimension=0, tiled=True))
    token_grad = jnp.concatenate(token_grad, axis=1)

    grad_in = mm(jnp.concatenate(rows_in, axis=1), d_joined, 0, 0)
    grad_out = mm(hidden, jnp.concatenate(rows_grad, axis=1), 0, 0)
    half_width = width // 2
    other = 1 - core

    def sum_cores(x, axis):
        keep = lax.dynamic_slice_in_dim(x, core * half_width, half_width, axis)
        send = lax.dynamic_slice_in_dim(x, other * half_width, half_width, axis)
        got = lax.ppermute(send, "dp", [(0, 1), (1, 0)])
        return (keep + got).astype(bf16)[None]

    return token_grad, sum_cores(grad_in, 0), sum_cores(grad_out, 1)


def solution(mesh):
    split = Mesh(mesh.devices.reshape(2, Z, X, Y), ("dp", "z", "x", "y"))
    hosts = ("z", "x", "y")
    rows = P(("dp",) + hosts, None)
    in_specs = (rows, rows, rows, rows, P(hosts, None, None), P(hosts, None, None))
    out_specs = (rows, P(hosts, "dp", None), P(hosts, None, "dp"))
    return jax.shard_map(body, mesh=split, in_specs=in_specs, out_specs=out_specs, check_vma=False)
```

time: 861 us -> 321 us (0.37); the launches traced: 848 us -> 320 us
  waiting for transfers between devices: 426 us -> 183 us
  starting transfers between devices: 165 us -> 28 us
  blocking collectives: 110 us -> 23.3 us
  local copies, waits for them, and re-layouts: 77.1 us -> 9.6 us
  matrix products: 31.4 us -> 51.4 us
  other arithmetic: 23.6 us -> 11.5 us
    ppermute x4 -> x2, waiting for transfers between devices: 253 us -> 3.75 us  [sum_cores(): got = lax.ppermute(send, 'dp', [(0, 1), (1, 0)])]
    all_to_all x2 -> x3, starting transfers between devices: 147 us -> 23 us  [swap_plane(): lax.all_to_all(x, ('x', 'y'), split_axis=0, concat_axis=0, tiled=True)]
    all_to_all x1 -> x0, blocking collectives: 110 us -> none  [body(): lax.all_to_all(send_grad, 'expert', split_axis=0, concat_axis=0, tiled=True)]
    all_to_all x2 -> x3, waiting for transfers between devices: 174 us -> 81.4 us  [swap_plane(): lax.all_to_all(x, ('x', 'y'), split_axis=0, concat_axis=0, tiled=True)]
    all_gather x0 -> x2, waiting for transfers between devices: none -> 72.2 us  [gather_z(): return lax.all_gather(x, 'z', axis=0, tiled=True)]
    gather x7 -> x0, local copies, waits for them, and re-layouts: 38.2 us -> none  [the longest x2 11.1 us: body(): send_grad = jnp.where(occupied[:, None], scaled[source], zero_value)]
    reduce_scatter x2 -> x1, waiting for transfers between devices: 0.01 us -> 23.9 us  [body(): lax.psum_scatter(part, 'z', scatter_dimension=0, tiled=True)]
    all_gather x0 -> x1, blocking collectives: none -> 23.3 us  [gather_z(): return lax.all_gather(x, 'z', axis=0, tiled=True)]
  transfers between devices with their start and end apart: 8 -> 8, of which waited for: 6 -> 7; matrix products, arithmetic and copies ran while one was open for 8% -> 15% of each run, Pallas kernels for 0% -> 0%
where the time goes in v1:
time: 321 us; the launch traced here: 320 us
  waiting for transfers between devices  183 us (57%)
  matrix products  51.4 us (16%)
  starting transfers between devices  28 us (9%)
  blocking collectives  23.3 us (7%)
  between operations  14 us (4%)
  other arithmetic  11.5 us (4%)
  local copies, waits for them, and re-layouts  9.6 us (3%)
    all_to_all x3, waiting for transfers between devices, swap_plane(): lax.all_to_all(x, ('x', 'y'), split_axis=0, concat_axis=0, tiled=True)  81.4 us
    all_gather x2, waiting for transfers between devices, gather_z(): return lax.all_gather(x, 'z', axis=0, tiled=True)  72.2 us
    dot_general x9, matrix products, mm(): lax.dot_general(a, b, (((ca,), (cb,)), ((), ())), preferred_element_type=...  51.4 us
    reduce_scatter x1, waiting for transfers between devices, body(): lax.psum_scatter(part, 'z', scatter_dimension=0, tiled=True)  23.9 us
    all_gather x1, blocking collectives, gather_z(): return lax.all_gather(x, 'z', axis=0, tiled=True)  23.3 us
    all_to_all x3, starting transfers between devices, swap_plane(): lax.all_to_all(x, ('x', 'y'), split_axis=0, concat_axis=0, tiled=True)  23 us
    broadcast_in_dim x2, other arithmetic, sum_cores(): return (keep + got).astype(bf16)[None]  7.52 us
  transfers between devices with their start and end apart: 8, of which 7 were waited for; matrix products, arithmetic and copies ran while one was open for 15% of the time, Pallas kernels for 0%

profile of v1, /device:TPU:1, one launch (start us, length us, event | category | flops | bytes accessed | tf_op | source)
XLA Modules:
  0.0 320.4 jit_solution(10744743611331638339)
XLA Ops:
  7.2 0.0 copy-start
  7.2 0.0 all-gather.5.cloned.1.call-start
  7.2 0.7 all-gather.5.cloned.1.call-update
  7.9 0.0 all-gather.3.cloned.1.call-start
  8.0 0.7 all-gather.3.cloned.1.call-update
  8.7 0.7 convert_element_type.42
  9.4 0.1 broadcast_bitcast_fusion
  9.5 0.1 eq.87
  9.5 0.1 eq.88
  9.6 0.7 maximum_bitcast_fusion
  10.3 23.3 %all_gather.9 = f32[64,128]{1,0:T(8,128)S(1)} all-gather(f32[8,128]{1,0:T(8,128)S(1)} %maximum_bitcast_fusion), channel_id=1, replica_groups=mesh['dp'=2,'z'=8,'x'=4,'y'=4] {'z'}, dimensions={0}, use_global_device_ids=true | all-gather | bytes 36864 | tf_op jit(solution)/shard_map/all_gather | solution.py:64
  33.7 0.1 compare_reduce_fusion
  33.8 0.1 convolution_select_fusion
  33.9 0.1 broadcast_select_fusion
  34.0 0.0 copy-start.3
  34.0 0.8 copy-done.3
  34.8 1.5 bitcast_compare_fusion
  36.3 32.3 %all-gather.5.cloned.1.call-done = bf16[1024,2048]{1,0:T(8,128)(2,1)} async-done(((bf16[128,2048]{1,0:T(8,128)(2,1)}), bf16[1024,2048]{1,0:T(8,128)(2,1)}) %all-gather.5.cloned.1.call-update) | async-done | bytes 4194320 | tf_op jit(solution)/shard_map/all_gather | solution.py:64
  68.6 8.2 %convolution_convert_fusion.2 = bf16[896,2048]{1,0:T(8,128)(2,1)} fusion(pred[896,1024]{1,0:T(32,128)(4,1)} %bitcast_compare_fusion, bf16[1024,2048]{1,0:T(8,128)(2,1)} %all-gather.5.cloned.1.call-done), kind=kOutput, calls=%fused_computation.4 | convolution fusion | flops 3759931392 | bytes 8781824 | tf_op jit(solution)/shard_map/dot_general | solution.py:19
  76.8 6.6 %all-to-all-start.1 = ((bf16[16,56,2048]{2,1,0:T(8,128)(2,1)}), bf16[16,56,2048]{2,1,0:T(8,128)(2,1)}, u32[]{:S(2)}, u32[]{:S(2)}) async-start(bf16[16,56,2048]{2,1,0:T(8,128)(2,1)} %bitcast.52), calls=%async_computation.1 | async-start | bytes 7340032 | tf_op jit(solution)/shard_map/all_to_all | solution.py:67
  83.4 0.1 fusion.10
  83.6 0.3 select_reduce_fusion
  83.9 0.1 mul.43
  83.9 39.9 %all-gather.3.cloned.1.call-done = bf16[1024,2048]{1,0:T(8,128)(2,1)} async-done(((bf16[128,2048]{1,0:T(8,128)(2,1)}), bf16[1024,2048]{1,0:T(8,128)(2,1)}) %all-gather.3.cloned.1.call-update) | async-done | bytes 4194320 | tf_op jit(solution)/shard_map/all_gather | solution.py:64
  123.8 8.2 %multiply_convert_fusion = bf16[896,2048]{1,0:T(8,128)(2,1)} fusion(pred[896,1024]{1,0:T(32,128)(4,1)} %bitcast_compare_fusion, bf16[1024,2048]{1,0:T(8,128)(2,1)} %all-gather.3.cloned.1.call-done, f32[896]{0:T(1024)S(1)} %mul.43), kind=kOutput, calls=%fused_computation | convolution fusion | flops 3761766400 | bytes 8785408 | tf_op jit(solution)/shard_map/dot_general | solution.py:19
  132.0 0.8 all-to-all-done.1
  132.8 11.7 %all-to-all-start = ((bf16[16,56,2048]{2,1,0:T(8,128)(2,1)}), bf16[16,56,2048]{2,1,0:T(8,128)(2,1)}, u32[]{:S(2)}, u32[]{:S(2)}) async-start(bf16[16,56,2048]{2,1,0:T(8,128)(2,1)} %bitcast.53), calls=%async_computation | async-start | bytes 7340032 | tf_op jit(solution)/shard_map/all_to_all | solution.py:67
  144.5 0.0 copy-done
  144.5 7.1 %fusion.1 = f32[896,768]{0,1:T(8,128)} fusion(bf16[896,2048]{1,0:T(8,128)(2,1)} %bitcast.11, bf16[1,2048,768]{2,1,0:T(8,128)(2,1)S(1)} %copy-done), kind=kOutput, calls=%fused_computation.6 | convolution fusion | flops 2818572288 | bytes 9568256 | tf_op jit(solution)/shard_map/dot_general | solution.py:19
  151.6 38.2 %all-to-all-done = bf16[16,56,2048]{2,1,0:T(8,128)(2,1)} async-done(((bf16[16,56,2048]{2,1,0:T(8,128)(2,1)}), bf16[16,56,2048]{2,1,0:T(8,128)(2,1)}, u32[]{:S(2)}, u32[]{:S(2)}) %all-to-all-start) | async-done | bytes 3670048 | tf_op jit(solution)/shard_map/all_to_all | solution.py:67
  189.8 5.4 %multiply_convert_fusion.3 = (bf16[896,384]{0,1:T(8,128)(2,1)S(1)}, bf16[896,384]{0,1:T(8,128)(2,1)S(1)}) fusion(f32[896,768]{0,1:T(8,128)} %fusion.1, bf16[896,2048]{1,0:T(8,128)(2,1)} %bitcast.8, bf16[1,384,2048]{2,1,0:T(8,128)(2,1)} %param.11), kind=kOutput, calls=%fused_computation.17 | convolution fusion | flops 1413758976 | bytes 9371648 | tf_op jit(solution)/shard_map/dot_general | solution.py:19
  195.2 0.0 copy-start.7
  195.2 0.0 copy-start.9
  195.2 4.6 %convolution_convert_fusion.1 = bf16[896,2048]{1,0:T(8,128)(2,1)} fusion(bf16[1,2048,768]{2,1,0:T(8,128)(2,1)S(1)} %copy-done, bf16[896,384]{0,1:T(8,128)(2,1)S(1)} %get-tuple-element.4, bf16[896,384]{0,1:T(8,128)(2,1)S(1)} %get-tuple-element.3), kind=kOutput, calls=%fused_computation.3 | convolution fusion | flops 2823159808 | bytes 8192000 | tf_op jit(solution)/shard_map/dot_general | solution.py:19
  199.8 0.0 copy-done.7
  199.8 0.0 copy-done.9
  199.8 0.0 copy-start.4
  199.8 4.6 %all-to-all-start.2 = ((bf16[16,56,2048]{2,1,0:T(8,128)(2,1)}), bf16[16,56,2048]{2,1,0:T(8,128)(2,1)}, u32[]{:S(2)}, u32[]{:S(2)}) async-start(bf16[16,56,2048]{2,1,0:T(8,128)(2,1)} %bitcast.54), calls=%async_computation.2 | async-start | bytes 7340032 | tf_op jit(solution)/shard_map/all_to_all | solution.py:67
  204.5 0.3 reduce-scatter.2.cloned.1.call-start
  204.7 0.0 copy-done.4
  204.7 0.6 broadcast_compare_fusion
  205.3 42.5 %all-to-all-done.2 = bf16[16,56,2048]{2,1,0:T(8,128)(2,1)} async-done(((bf16[16,56,2048]{2,1,0:T(8,128)(2,1)}), bf16[16,56,2048]{2,1,0:T(8,128)(2,1)}, u32[]{:S(2)}, u32[]{:S(2)}) %all-to-all-start.2) | async-done | bytes 3670048 | tf_op jit(solution)/shard_map/all_to_all | solution.py:67
  247.8 8.2 %convolution_convert_fusion = bf16[1024,2048]{1,0:T(8,128)(2,1)} fusion(pred[896,1024]{1,0:T(8,128)(4,1)S(1)} %bitcast.55, bf16[896,2048]{1,0:T(8,128)(2,1)} %bitcast.14), kind=kOutput, calls=%fused_computation.1 | convolution fusion | flops 3760193536 | bytes 8781824 | tf_op jit(solution)/shard_map/dot_general | solution.py:19
  256.0 0.0 reduce-scatter.2.cloned.1.call-update
  256.1 1.1 copy-done.8
  257.1 0.2 copy-done.10
  257.3 5.6 %fusion.7 = f32[2048,768]{1,0:T(8,128)S(1)} fusion(bf16[896,2048]{1,0:T(8,128)(2,1)} %bitcast.11, bf16[896,384]{0,1:T(8,128)(2,1)S(1)} %copy-done.10, bf16[896,384]{0,1:T(8,128)(2,1)S(1)} %copy-done.8), kind=kOutput, calls=%fused_computation.21 | convolution fusion | flops 2821324800 | bytes 11337728 | tf_op jit(solution)/shard_map/dot_general | solution.py:19
  262.9 0.0 copy-start.2
  263.0 0.0 copy-start.6
  263.0 1.8 constant_dynamic-slice_fusion.1
  264.8 2.2 copy-done.2
  267.0 4.7 %collective-permute-start = (f32[1024,768]{1,0:T(8,128)}, f32[1024,768]{1,0:T(8,128)}, u32[]{:S(2)}, u32[]{:S(2)}) collective-permute-start(f32[1024,768]{1,0:T(8,128)} %constant_dynamic-slice_fusion.1), channel_id=1, source_target_pairs={{0,128},{128,0},{1,129},{129,1},{2,130},{130,2},{3,131},{131,3},{4... | collective-permute-start | bytes 9437192 | tf_op jit(solution)/shard_map/ppermute | solution.py:103
  271.7 0.0 copy-done.6
  271.7 3.9 %fusion.9 = f32[384,2048]{1,0:T(8,128)S(1)} fusion(bf16[896,2048]{1,0:T(8,128)(2,1)} %bitcast.8, f32[896,768]{0,1:T(8,128)S(1)} %copy-done.6), kind=kOutput, calls=%fused_computation.23 | convolution fusion | flops 1411350528 | bytes 9568256 | tf_op jit(solution)/shard_map/dot_general | solution.py:19
  275.6 0.0 copy-start.5
  275.6 1.8 copy-done.5
  277.4 1.3 constant_dynamic-slice_fusion
  278.7 0.0 collective-permute-start.1
  278.7 3.7 %collective-permute-done.1 = f32[384,1024]{1,0:T(8,128)} collective-permute-done((f32[384,1024]{1,0:T(8,128)}, f32[384,1024]{1,0:T(8,128)}, u32[]{:S(2)}, u32[]{:S(2)}) %collective-permute-start.1) | collective-permute-done | bytes 1572896 | tf_op jit(solution)/shard_map/ppermute | solution.py:103
  282.4 3.2 fusion.8
  285.6 0.0 collective-permute-done
  285.6 4.4 %fusion.3 = bf16[1,1024,768]{2,1,0:T(8,128)(2,1)} fusion(f32[1024,768]{1,0:T(8,128)} %collective-permute-done, f32[2048,768]{1,0:T(8,128)} %copy-done.2, s32[]{:T(128)S(6)} %select_n.37), kind=kLoop, calls=%fused_computation.10 | loop fusion | flops 1572864 | bytes 7864324 | tf_op jit(solution)/shard_map/broadcast_in_dim | solution.py:104
  290.0 23.9 %reduce-scatter.2.cloned.1.call-done = bf16[128,2048]{1,0:T(8,128)(2,1)} async-done(((bf16[1024,2048]{1,0:T(8,128)(2,1)}), bf16[128,2048]{1,0:T(8,128)(2,1)}) %reduce-scatter.2.cloned.1.call-update) | async-done | bytes 524304 | tf_op jit(solution)/shard_map/reduce_scatter | solution.py:92
  313.8 0.0 copy-done.1
  (11 shorter events, 0.1 us)
Async XLA Ops:
  7.2 137.4 %copy-start = (bf16[1,2048,768]{2,1,0:T(8,128)(2,1)S(1)}, bf16[1,2048,768]{2,1,0:T(8,128)(2,1)}, u32[]{:S(2)}) copy-start(bf16[1,2048,768]{2,1,0:T(8,128)(2,1)} %param.10) | copy-start | bytes 9437188
  7.2 61.4 %all-gather.5.cloned.1.call-start = ((), (), s32[]{:S(2)}) async-start(), calls=%async_computation.5 | async-start | bytes 4718592 | tf_op jit(solution)/shard_map/all_gather | solution.py:64
  7.9 115.9 %all-gather.3.cloned.1.call-start = ((), (), s32[]{:S(2)}) async-start(), calls=%async_computation.4 | async-start | bytes 4718592 | tf_op jit(solution)/shard_map/all_gather | solution.py:64
  34.0 0.8 copy-start.3
  76.8 56.0 %all-to-all-start.1 = ((bf16[16,56,2048]{2,1,0:T(8,128)(2,1)}), bf16[16,56,2048]{2,1,0:T(8,128)(2,1)}, u32[]{:S(2)}, u32[]{:S(2)}) async-start(bf16[16,56,2048]{2,1,0:T(8,128)(2,1)} %bitcast.52), calls=%async_computation.1 | async-start | bytes 7340032 | tf_op jit(solution)/shard_map/all_to_all | solution.py:67
  132.8 57.0 %all-to-all-start = ((bf16[16,56,2048]{2,1,0:T(8,128)(2,1)}), bf16[16,56,2048]{2,1,0:T(8,128)(2,1)}, u32[]{:S(2)}, u32[]{:S(2)}) async-start(bf16[16,56,2048]{2,1,0:T(8,128)(2,1)} %bitcast.53), calls=%async_computation | async-start | bytes 7340032 | tf_op jit(solution)/shard_map/all_to_all | solution.py:67
  195.2 4.6 %copy-start.7 = (bf16[896,384]{0,1:T(8,128)(2,1)}, bf16[896,384]{0,1:T(8,128)(2,1)S(1)}, u32[]{:S(2)}) copy-start(bf16[896,384]{0,1:T(8,128)(2,1)S(1)} %get-tuple-element.3) | copy-start | bytes 2064388
  195.2 4.6 %copy-start.9 = (bf16[896,384]{0,1:T(8,128)(2,1)}, bf16[896,384]{0,1:T(8,128)(2,1)S(1)}, u32[]{:S(2)}) copy-start(bf16[896,384]{0,1:T(8,128)(2,1)S(1)} %get-tuple-element.4) | copy-start | bytes 2064388
  199.8 4.9 %copy-start.4 = (f32[16,8,1024]{2,1,0:T(8,128)S(1)}, f32[16,8,1024]{2,1,0:T(8,128)}, u32[]{:S(2)}) copy-start(f32[16,8,1024]{2,1,0:T(8,128)} %copy-done.3) | copy-start | bytes 1572868
  199.8 48.0 %all-to-all-start.2 = ((bf16[16,56,2048]{2,1,0:T(8,128)(2,1)}), bf16[16,56,2048]{2,1,0:T(8,128)(2,1)}, u32[]{:S(2)}, u32[]{:S(2)}) async-start(bf16[16,56,2048]{2,1,0:T(8,128)(2,1)} %bitcast.54), calls=%async_computation.2 | async-start | bytes 7340032 | tf_op jit(solution)/shard_map/all_to_all | solution.py:67
  204.5 109.4 %reduce-scatter.2.cloned.1.call-start = ((), (), s32[]{:S(2)}) async-start(), calls=%async_computation.6 | async-start | bytes 4718592 | tf_op jit(solution)/shard_map/reduce_scatter | solution.py:92
  256.0 1.1 copy-start.8
  256.0 1.3 copy-start.10
  262.9 4.0 %copy-start.2 = (f32[2048,768]{1,0:T(8,128)}, f32[2048,768]{1,0:T(8,128)S(1)}, u32[]{:S(2)}) copy-start(f32[2048,768]{1,0:T(8,128)S(1)} %fusion.7) | copy-start | bytes 18874372
  263.0 8.7 %copy-start.6 = (f32[896,768]{0,1:T(8,128)S(1)}, f32[896,768]{0,1:T(8,128)}, u32[]{:S(2)}) copy-start(f32[896,768]{0,1:T(8,128)} %fusion.1) | copy-start | bytes 8257540
  267.0 18.6 %collective-permute-start = (f32[1024,768]{1,0:T(8,128)}, f32[1024,768]{1,0:T(8,128)}, u32[]{:S(2)}, u32[]{:S(2)}) collective-permute-start(f32[1024,768]{1,0:T(8,128)} %constant_dynamic-slice_fusion.1), channel_id=1, source_target_pairs={{0,128},{128,0},{1,129},{129,1},{2,130},{130,2},{3,131},{131,3},{4... | collective-permute-start | bytes 9437192 | tf_op jit(solution)/shard_map/ppermute | solution.py:103
  275.6 1.8 copy-start.5
  278.7 3.8 %collective-permute-start.1 = (f32[384,1024]{1,0:T(8,128)}, f32[384,1024]{1,0:T(8,128)}, u32[]{:S(2)}, u32[]{:S(2)}) collective-permute-start(f32[384,1024]{1,0:T(8,128)} %constant_dynamic-slice_fusion), channel_id=1, source_target_pairs={{0,128},{128,0},{1,129},{129,1},{2,130},{130,2},{3,131},{131,3},{4... | collective-permute-start | bytes 4718600 | tf_op jit(solution)/shard_map/ppermute | solution.py:103
  282.4 31.4 %copy-start.1 = (bf16[1,2048,768]{2,1,0:T(8,128)(2,1)S(1)}, bf16[1,2048,768]{2,1,0:T(8,128)(2,1)}, u32[]{:S(2)}) copy-start(bf16[1,2048,768]{2,1,0:T(8,128)(2,1)} %param.10) | copy-start | bytes 9437188
Sparse Core Ops, SparseCore 0:
  9.8 58.7 all-gather.4
  70.4 53.4 all-gather.2
  256.2 57.6 reduce-scatter.1

commit v2 on v1

v2 whole, which is shorter than its diff:
```python
import jax
import jax.numpy as jnp
from jax import lax
from jax.experimental import pallas as pl
from jax.experimental.pallas import tpu as pltpu
from jax.sharding import Mesh
from jax.sharding import PartitionSpec as P

Z, X, Y = 8, 4, 4
PLANE = X * Y
CAP = 7
SLOTS = PLANE * CAP * Z
GRAD_FIRST = 512

f32 = jnp.float32
bf16 = jnp.bfloat16


def mm(a, b, ca, cb):
    return lax.dot_general(a, b, (((ca,), (cb,)), ((), ())), preferred_element_type=f32)


def silu_parts(gate_part):
    sigma = 1.0 / (1.0 + jnp.exp(-gate_part))
    return gate_part * sigma, sigma * (1.0 + gate_part * (1.0 - sigma))


def rank_table(ids, gates, local):
    sources, _, tok = ids.shape
    match = ids[:, :, None, :] == local[None, None, :, None]
    named = jnp.any(match, axis=1)
    gate = jnp.sum(jnp.where(match, gates[:, :, None, :], 0.0), axis=1)
    index = jnp.arange(tok, dtype=jnp.int32)
    earlier = (index[:, None] < index[None, :]).astype(bf16)
    before = mm(named.astype(bf16).reshape(-1, tok), earlier, 1, 0)
    return jnp.where(named, before.reshape(named.shape), -1.0), gate


def plane_slots(meta, plane):
    tok = meta.shape[-1]
    meta = meta.reshape(Z, 8, tok)
    local = plane * PLANE + jnp.arange(PLANE, dtype=jnp.int32)
    rank, gate = rank_table(meta[:, :4].astype(jnp.int32), meta[:, 4:], local)
    rank, gate = rank.transpose(1, 0, 2), gate.transpose(1, 0, 2)
    slot_rank = jnp.arange(CAP, dtype=jnp.int32).astype(f32)
    hit = rank[:, None] == slot_rank[None, :, None, None]
    slot_gate = jnp.sum(jnp.where(hit, gate[:, None], 0.0), axis=3).reshape(-1, 1)
    same = jnp.arange(Z)[:, None] == jnp.arange(Z)[None, :]
    wide = jnp.where(same[None, :, :, None], rank[:, None], -1.0).reshape(PLANE, 1, Z, Z * tok)
    slots = (wide == slot_rank[None, :, None, None]).astype(bf16)
    return slots.reshape(SLOTS, Z * tok), slot_gate


def column_slots(ids, gates):
    tok = ids.shape[-1]
    rank, gate = rank_table(ids[None], gates[None], jnp.arange(Z * PLANE, dtype=jnp.int32))
    rank = rank.reshape(Z, PLANE, tok).transpose(1, 0, 2)
    gate = gate.reshape(Z, PLANE, tok).transpose(1, 0, 2)
    slot_rank = jnp.arange(CAP, dtype=jnp.int32).astype(f32)
    hit = rank[:, None] == slot_rank[None, :, None, None]
    slot_gate = jnp.sum(jnp.where(hit, gate[:, None], 0.0), axis=3).reshape(-1, 1)
    return hit.astype(bf16).reshape(SLOTS, tok), slot_gate


def order_matrices(plane):
    rows = PLANE * CAP
    by_distance = lax.broadcasted_iota(jnp.int32, (SLOTS, SLOTS), 0)
    by_plane = lax.broadcasted_iota(jnp.int32, (SLOTS, SLOTS), 1)
    same_row = by_plane // Z == by_distance % rows
    at = by_plane % Z
    distance = by_distance // rows
    to_send = same_row & (at == (plane + distance) % Z)
    by_plane, by_distance = by_distance, by_plane
    received = (by_plane // Z == by_distance % rows) & (by_plane % Z == (plane + Z - by_distance // rows) % Z)
    return to_send.astype(bf16), received.astype(bf16)


def times(name, matrix, parts, tile):
    width = parts[0].shape[1]

    def kernel(matrix_ref, *refs):
        stacked = jnp.concatenate([ref[...] for ref in refs[:-1]], axis=0)
        refs[-1][...] = jnp.dot(matrix_ref[...], stacked, preferred_element_type=f32).astype(bf16)

    return pl.pallas_call(
        kernel,
        grid=(width // tile,),
        in_specs=[pl.BlockSpec(matrix.shape, lambda i: (0, 0))] + [pl.BlockSpec((p.shape[0], tile), lambda i: (0, i)) for p in parts],
        out_specs=pl.BlockSpec((matrix.shape[0], tile), lambda i: (0, i)),
        out_shape=jax.ShapeDtypeStruct((matrix.shape[0], width), bf16),
        compiler_params=pltpu.CompilerParams(vmem_limit_bytes=24 * 2**20),
        name=name,
    )(matrix, *parts)


def weave(received, parts):
    return times("weave", received, parts, 512)


def body(tokens, out_grad, expert_ids, gate_weights, w_in, w_out):
    width = tokens.shape[1]
    w_in, w_out = w_in[0], w_out[0]
    half = w_out.shape[0]
    plane = lax.axis_index("z")
    core = lax.axis_index("dp")

    def gather_z(x):
        return lax.all_gather(x, "z", axis=0, tiled=True)

    def swap_plane(x):
        return lax.all_to_all(x, ("x", "y"), split_axis=0, concat_axis=0, tiled=True)

    def swap_z(x):
        rows = PLANE * CAP
        parts = [x[:rows]]
        for distance in range(1, Z):
            piece = x[distance * rows : (distance + 1) * rows]
            parts.append(lax.ppermute(piece, "z", [(i, (i + distance) % Z) for i in range(Z)]))
        return parts

    ids = expert_ids.T
    gates = gate_weights.T
    own_slots, own_gate = lax.optimization_barrier(column_slots(ids, gates))
    to_send, received = lax.optimization_barrier(order_matrices(plane))

    tokens_all = gather_z(tokens)
    first = (mm(own_slots, out_grad[:, :GRAD_FIRST], 1, 0) * own_gate).astype(bf16)
    meta = jnp.concatenate([ids.astype(f32), gates], axis=0)
    meta, rest = lax.optimization_barrier((meta, out_grad[:, GRAD_FIRST:], first))[:2]
    first = swap_plane(first)
    meta = gather_z(meta)
    grads_all = gather_z(rest)
    first = mm(to_send, first, 1, 0).astype(bf16)
    meta, first = lax.optimization_barrier((meta, first))
    slots, slot_gate = lax.optimization_barrier(plane_slots(meta, plane))
    first = swap_z(lax.optimization_barrier((first, grads_all))[0])
    rows_in = mm(slots, tokens_all, 1, 0).astype(bf16)
    rows_in = swap_plane(rows_in)
    second = (mm(slots, grads_all, 1, 0) * slot_gate).astype(bf16)
    second = lax.optimization_barrier((second, first[1], first[2], rows_in))[0]
    second = swap_plane(second)
    first = weave(received, first)

    joined = mm(rows_in, w_in, 1, 0)
    d_hidden = mm(first, w_out[:, :GRAD_FIRST], 1, 1) + mm(second, w_out[:, GRAD_FIRST:], 1, 1)
    gate_part, up_part = joined[:, :half], joined[:, half:]
    activated, derivative = silu_parts(gate_part)
    hidden = (activated * up_part).astype(bf16)
    d_joined = jnp.concatenate([d_hidden * up_part * derivative, d_hidden * activated], axis=1).astype(bf16)

    back = swap_plane(mm(d_joined, w_in, 1, 1).astype(bf16))
    part = mm(slots, back, 0, 0).astype(bf16)
    token_grad = lax.psum_scatter(part, "z", scatter_dimension=0, tiled=True)

    grad_in = mm(rows_in, d_joined, 0, 0)
    grad_out = mm(hidden, jnp.concatenate([first, second], axis=1), 0, 0)
    half_width = width // 2
    other = 1 - core

    def sum_cores(x, axis):
        keep = lax.dynamic_slice_in_dim(x, core * half_width, half_width, axis)
        send = lax.dynamic_slice_in_dim(x, other * half_width, half_width, axis)
        got = lax.ppermute(send, "dp", [(0, 1), (1, 0)])
        return (keep + got).astype(bf16)[None]

    w_in_grad = sum_cores(grad_in, 0)
    w_out_grad = sum_cores(grad_out, 1)
    return token_grad, w_in_grad, w_out_grad


def solution(mesh):
    split = Mesh(mesh.devices.reshape(2, Z, X, Y), ("dp", "z", "x", "y"))
    hosts = ("z", "x", "y")
    rows = P(("dp",) + hosts, None)
    in_specs = (rows, rows, rows, rows, P(hosts, None, None), P(hosts, None, None))
    out_specs = (rows, P(hosts, "dp", None), P(hosts, None, "dp"))
    return jax.shard_map(body, mesh=split, in_specs=in_specs, out_specs=out_specs, check_vma=False)
```

time: 321 us -> 304 us (0.947)
  waiting for transfers between devices: 183 us -> 88.8 us
  blocking collectives: 23.3 us -> 73.9 us
  starting transfers between devices: 28 us -> 41.4 us
  other arithmetic: 11.5 us -> 16.2 us
  local copies, waits for them, and re-layouts: 9.6 us -> 14.2 us
    all_to_all x3, waiting for transfers between devices: 81.4 us -> 6.15 us  [swap_plane(): lax.all_to_all(x, ('x', 'y'), split_axis=0, concat_axis=0, tiled=True)]
    all_to_all x0 -> x1, blocking collectives: none -> 49.6 us  [swap_plane(): lax.all_to_all(x, ('x', 'y'), split_axis=0, concat_axis=0, tiled=True)]
    all_gather x2, waiting for transfers between devices: 72.2 us -> 42.2 us  [gather_z(): return lax.all_gather(x, 'z', axis=0, tiled=True)]
    ppermute x0 -> x7, waiting for transfers between devices: none -> 15.2 us  [swap_z(): lax.ppermute(piece, 'z', [(i, (i + distance) % Z) for i in range(Z)])]
    ppermute x0 -> x7, starting transfers between devices: none -> 11.6 us  [swap_z(): lax.ppermute(piece, 'z', [(i, (i + distance) % Z) for i in range(Z)])]
    convert_element_type x2 -> x5, other arithmetic: 0.69 us -> 6.18 us  [the longest x1 4.39 us: order_matrices(): return (to_send.astype(bf16), received.astype(bf16))]
    slice x0 -> x2, local copies, waits for them, and re-layouts: none -> 3.81 us  [the longest x1 2.04 us: swap_z(): piece = x[distance * rows:(distance + 1) * rows]]
    dot_general x9 -> x13, matrix products: 51.4 us -> 53.3 us  [mm(): lax.dot_general(a, b, (((ca,), (cb,)), ((), ())), preferred_element_type=...]
  transfers between devices with their start and end apart: 8 -> 15, of which waited for: 7 -> 9; matrix products, arithmetic and copies ran while one was open for 15% -> 20% of each run, Pallas kernels for 0% -> 0%
where the time goes in v2:
time: 304 us; the launch traced here: 303 us
  waiting for transfers between devices  88.8 us (29%)
  blocking collectives  73.9 us (24%)
  matrix products  53.3 us (18%)
  starting transfers between devices  41.4 us (14%)
  other arithmetic  16.2 us (5%)
  local copies, waits for them, and re-layouts  14.2 us (5%)
  between operations  14.1 us (5%)
    dot_general x13, matrix products, mm(): lax.dot_general(a, b, (((ca,), (cb,)), ((), ())), preferred_element_type=...  53.3 us
    all_to_all x1, blocking collectives, swap_plane(): lax.all_to_all(x, ('x', 'y'), split_axis=0, concat_axis=0, tiled=True)  49.6 us
    all_gather x2, waiting for transfers between devices, gather_z(): return lax.all_gather(x, 'z', axis=0, tiled=True)  42.2 us
    all_to_all x3, starting transfers between devices, swap_plane(): lax.all_to_all(x, ('x', 'y'), split_axis=0, concat_axis=0, tiled=True)  26 us
    all_gather x1, blocking collectives, gather_z(): return lax.all_gather(x, 'z', axis=0, tiled=True)  24.3 us
    reduce_scatter x1, waiting for transfers between devices, body(): token_grad = lax.psum_scatter(part, 'z', scatter_dimension=0, tiled=True)  21.4 us
    ppermute x7, waiting for transfers between devices, swap_z(): lax.ppermute(piece, 'z', [(i, (i + distance) % Z) for i in range(Z)])  15.2 us
    ppermute x7, starting transfers between devices, swap_z(): lax.ppermute(piece, 'z', [(i, (i + distance) % Z) for i in range(Z)])  11.6 us
  transfers between devices with their start and end apart: 15, of which 9 were waited for; matrix products, arithmetic and copies ran while one was open for 20% of the time, Pallas kernels for 0%

profile of v2, /device:TPU:1, one launch (start us, length us, event | category | flops | bytes accessed | tf_op | source)
XLA Modules:
  0.0 303.1 jit_solution(12911101482394824331)
XLA Ops:
  7.2 0.7 all-gather.5.cloned.1.call-update
  7.9 0.9 fusion.25
  8.8 0.1 convolution_select_fusion.1
  9.0 0.1 eq.139
  9.1 0.1 eq.140
  9.1 0.7 select_reduce_fusion.2
  9.9 0.3 select_reduce_fusion.1
  10.2 0.1 reshape.107
  10.3 0.2 fusion.22
  10.5 2.2 multiply_convert_fusion.1
  12.7 7.6 %all-to-all-start = ((bf16[16,56,512]{2,1,0:T(8,128)(2,1)}), bf16[16,56,512]{2,1,0:T(8,128)(2,1)}, u32[]{:S(2)}, u32[]{:S(2)}) async-start(bf16[16,56,512]{2,1,0:T(8,128)(2,1)} %bitcast.69), calls=%async_computation | async-start | bytes 1835008 | tf_op jit(solution)/shard_map/all_to_all | solution.py:111
  20.4 1.8 slice.48
  22.3 4.4 %fusion.11 = (bf16[896,896]{1,0:T(8,128)(2,1)}, bf16[896,896]{1,0:T(8,128)(2,1)}) fusion(s32[896]{0:T(1024)S(1)} %get-tuple-element.44, s32[896]{0:T(1024)S(1)} %get-tuple-element.51, s32[]{:T(128)S(6)} %add.87, s32[896]{0:T(1024)S(1)} %get-tuple-element.42, s32[896]{0:T(1024)S(1)} %get-tuple-element.43, s32[896]{0:T(1024)S(1)} %get-tuple-element.49, ...), kind=kLoop, calls=%fused_computation.24 | loop fusion | flops 32112640 | bytes 3243528 | tf_op jit(solution)/shard_map/convert_element_type | solution.py:75
  26.7 0.1 broadcast_bitcast_fusion
  26.8 24.3 %all_gather.9 = f32[64,128]{1,0:T(8,128)S(1)} all-gather(f32[8,128]{1,0:T(8,128)S(1)} %pad_maximum_fusion.3), channel_id=1, replica_groups=mesh['dp'=2,'z'=8,'x'=4,'y'=4] {'z'}, dimensions={0}, use_global_device_ids=true | all-gather | bytes 36864 | tf_op jit(solution)/shard_map/all_gather | solution.py:108
  51.1 3.7 %convolution_convert_fusion.3 = bf16[896,512]{1,0:T(8,128)(2,1)} fusion(bf16[896,896]{1,0:T(8,128)(2,1)} %get-tuple-element.18, bf16[896,512]{1,0:T(8,128)(2,1)} %bitcast.8), kind=kOutput, calls=%fused_computation.33 | convolution fusion | flops 822542336 | bytes 3440640 | tf_op jit(solution)/shard_map/dot_general | solution.py:20
  54.8 0.1 fusion.24
  55.0 0.1 compare_reduce_fusion
  55.1 0.1 convolution_select_fusion
  55.2 0.3 select_reduce_fusion
  55.5 0.1 reshape.109
  55.7 1.6 fusion.4
  57.3 11.5 %all-gather.5.cloned.1.call-done = bf16[1024,2048]{1,0:T(8,128)(2,1)} async-done(((bf16[128,2048]{1,0:T(8,128)(2,1)}), bf16[1024,2048]{1,0:T(8,128)(2,1)}) %all-gather.5.cloned.1.call-update) | async-done | bytes 4194320 | tf_op jit(solution)/shard_map/all_gather | solution.py:108
  68.8 8.5 %convolution_convert_fusion.2 = bf16[896,2048]{1,0:T(8,128)(2,1)} fusion(bf16[896,1024]{1,0:T(8,128)(2,1)} %fusion.4, bf16[1024,2048]{1,0:T(8,128)(2,1)} %all-gather.5.cloned.1.call-done), kind=kOutput, calls=%fused_computation.15 | convolution fusion | flops 3759931392 | bytes 9699328 | tf_op jit(solution)/shard_map/dot_general | solution.py:20
  77.3 6.6 %all-to-all-start.1 = ((bf16[16,56,2048]{2,1,0:T(8,128)(2,1)}), bf16[16,56,2048]{2,1,0:T(8,128)(2,1)}, u32[]{:S(2)}, u32[]{:S(2)}) async-start(bf16[16,56,2048]{2,1,0:T(8,128)(2,1)} %bitcast.66), calls=%async_computation.1 | async-start | bytes 7340032 | tf_op jit(solution)/shard_map/all_to_all | solution.py:111
  83.9 30.6 %all-gather.3.cloned.1.call-done = bf16[1024,1536]{1,0:T(8,128)(2,1)} async-done(((bf16[128,1536]{1,0:T(8,128)(2,1)}), bf16[1024,1536]{1,0:T(8,128)(2,1)}) %all-gather.3.cloned.1.call-update) | async-done | bytes 3145744 | tf_op jit(solution)/shard_map/all_gather | solution.py:108
  114.5 2.0 fusion.45
  116.6 1.6 collective-permute-start.1
  118.2 1.6 collective-permute-start
  119.8 7.1 %multiply_convert_fusion = bf16[896,1536]{1,0:T(8,128)(2,1)} fusion(bf16[896,1024]{1,0:T(8,128)(2,1)} %fusion.4, bf16[1024,1536]{1,0:T(8,128)(2,1)} %all-gather.3.cloned.1.call-done, f32[896]{0:T(1024)S(1)} %reduce.3), kind=kOutput, calls=%fused_computation | convolution fusion | flops 2821324800 | bytes 7736832 | tf_op jit(solution)/shard_map/dot_general | solution.py:20
  126.9 6.1 %all-to-all-done.1 = bf16[16,56,2048]{2,1,0:T(8,128)(2,1)} async-done(((bf16[16,56,2048]{2,1,0:T(8,128)(2,1)}), bf16[16,56,2048]{2,1,0:T(8,128)(2,1)}, u32[]{:S(2)}, u32[]{:S(2)}) %all-to-all-start.1) | async-done | bytes 3670048 | tf_op jit(solution)/shard_map/all_to_all | solution.py:111
  133.0 11.8 %all-to-all-start.2 = ((bf16[16,56,1536]{2,1,0:T(8,128)(2,1)}), bf16[16,56,1536]{2,1,0:T(8,128)(2,1)}, u32[]{:S(2)}, u32[]{:S(2)}) async-start(bf16[16,56,1536]{2,1,0:T(8,128)(2,1)} %bitcast.70), calls=%async_computation.2 | async-start | bytes 5505024 | tf_op jit(solution)/shard_map/all_to_all | solution.py:111
  144.8 1.2 collective-permute-start.6
  146.1 1.9 collective-permute-start.5
  148.0 2.2 collective-permute-start.4
  150.1 2.4 collective-permute-start.3
  152.5 0.8 collective-permute-start.2
  153.3 1.5 collective-permute-done.5.refs_6_
  154.8 2.5 collective-permute-done.4.refs_5_
  157.3 2.2 collective-permute-done.3.refs_4_
  159.5 9.0 %collective-permute-done.2.refs_3_ = bf16[112,512]{1,0:T(8,128)(2,1)S(1)} collective-permute-done((bf16[112,512]{1,0:T(8,128)(2,1)}, bf16[112,512]{1,0:T(8,128)(2,1)S(1)}, u32[]{:S(2)}, u32[]{:S(2)}) %collective-permute-start.2) | collective-permute-done | bytes 114720 | tf_op jit(solution)/shard_map/ppermute | solution.py:118
  168.5 1.4 copy-done.2
  169.9 1.1 weave.1
  171.1 0.9 copy-done.3
  172.0 7.1 %fusion.14 = f32[896,768]{0,1:T(8,128)} fusion(bf16[896,2048]{1,0:T(8,128)(2,1)} %bitcast.16, bf16[1,2048,768]{2,1,0:T(8,128)(2,1)S(1)} %copy-done), kind=kOutput, calls=%fused_computation.27 | convolution fusion | flops 2818572288 | bytes 9568256 | tf_op jit(solution)/shard_map/dot_general | solution.py:20
  179.1 3.7 %fusion.18 = f32[896,384]{0,1:T(8,128)S(1)} fusion(bf16[896,1536]{1,0:T(8,128)(2,1)} %bitcast.18, bf16[384,2048]{1,0:T(8,128)(2,1)} %bitcast.81), kind=kOutput, calls=%fused_computation.41 | convolution fusion | flops 1056964608 | bytes 5308416 | tf_op jit(solution)/shard_map/dot_general | solution.py:20
  182.7 2.0 multiply_convert_fusion.4
  184.7 3.3 %convolution_convert_fusion.1 = bf16[896,2048]{1,0:T(8,128)(2,1)S(1)} fusion(bf16[1,2048,768]{2,1,0:T(8,128)(2,1)S(1)} %copy-done, bf16[896,384]{0,1:T(8,128)(2,1)S(1)} %get-tuple-element.28, bf16[896,384]{0,1:T(8,128)(2,1)S(1)} %get-tuple-element.27), kind=kOutput, calls=%fused_computation.14 | convolution fusion | flops 2823159808 | bytes 8192000 | tf_op jit(solution)/shard_map/dot_general | solution.py:20
  188.1 49.6 %all_to_all.48 = bf16[16,56,2048]{2,1,0:T(8,128)(2,1)S(1)} all-to-all(bf16[16,56,2048]{2,1,0:T(8,128)(2,1)S(1)} %bitcast.68), channel_id=1, replica_groups=mesh['dp'=2,'z'=8,'x'=4,'y'=4] {'x','y'}, dimensions={0} | all-to-all | bytes 7340032 | tf_op jit(solution)/shard_map/all_to_all | solution.py:111
  237.8 6.2 %convolution_convert_fusion = bf16[1024,2048]{1,0:T(8,128)(2,1)} fusion(bf16[896,1024]{1,0:T(8,128)(2,1)S(1)} %copy-done.8, bf16[896,2048]{1,0:T(8,128)(2,1)S(1)} %bitcast.67), kind=kOutput, calls=%fused_computation.7 | convolution fusion | flops 3760193536 | bytes 9699328 | tf_op jit(solution)/shard_map/dot_general | solution.py:20
  244.0 1.1 copy-done.14
  245.1 0.2 copy-done.16
  245.3 5.6 %fusion.20 = f32[2048,768]{1,0:T(8,128)S(1)} fusion(bf16[896,2048]{1,0:T(8,128)(2,1)} %bitcast.16, bf16[896,384]{0,1:T(8,128)(2,1)S(1)} %copy-done.16, bf16[896,384]{0,1:T(8,128)(2,1)S(1)} %copy-done.14), kind=kOutput, calls=%fused_computation.45 | convolution fusion | flops 2821324800 | bytes 11337728 | tf_op jit(solution)/shard_map/dot_general | solution.py:20
  250.9 1.8 constant_dynamic-slice_fusion.1
  252.8 2.6 copy-done.6
  255.3 3.2 %collective-permute-start.7 = (f32[1024,768]{1,0:T(8,128)}, f32[1024,768]{1,0:T(8,128)}, u32[]{:S(2)}, u32[]{:S(2)}) collective-permute-start(f32[1024,768]{1,0:T(8,128)} %constant_dynamic-slice_fusion.1), channel_id=1, source_target_pairs={{0,128},{128,0},{1,129},{129,1},{2,130},{130,2},{3,131},{131,3},{4... | collective-permute-start | bytes 9437192 | tf_op jit(solution)/shard_map/ppermute | solution.py:163
  258.5 3.6 %fusion = f32[384,2048]{1,0:T(8,128)S(1)} fusion(bf16[896,1536]{1,0:T(8,128)(2,1)} %bitcast.18, bf16[896,512]{1,0:T(8,128)(2,1)S(1)} %copy-done.5, f32[896,768]{0,1:T(8,128)S(1)} %copy-done.12), kind=kOutput, calls=%fused_computation.8 | convolution fusion | flops 1418690560 | bytes 9568256 | tf_op jit(solution)/shard_map/dot_general | solution.py:20
  262.1 1.6 copy-done.7
  263.8 0.2 constant_dynamic-slice_fusion
  263.9 0.5 collective-permute-start.8
  264.4 3.2 %collective-permute-done.8 = f32[384,1024]{1,0:T(8,128)} collective-permute-done((f32[384,1024]{1,0:T(8,128)S(1)}, f32[384,1024]{1,0:T(8,128)}, u32[]{:S(2)}, u32[]{:S(2)}) %collective-permute-start.8) | collective-permute-done | bytes 1572896 | tf_op jit(solution)/shard_map/ppermute | solution.py:163
  267.6 3.2 %fusion.21 = bf16[1,384,1024]{2,1,0:T(8,128)(2,1)} fusion(f32[384,1024]{1,0:T(8,128)} %collective-permute-done.8, f32[384,2048]{1,0:T(8,128)} %copy-done.7, s32[]{:T(128)S(6)} %select_n.111), kind=kLoop, calls=%fused_computation.46 | loop fusion | flops 786432 | bytes 3932164 | tf_op jit(solution)/shard_map/broadcast_in_dim | solution.py:164
  270.8 4.4 %fusion.16 = bf16[1,1024,768]{2,1,0:T(8,128)(2,1)} fusion(f32[1024,768]{1,0:T(8,128)} %collective-permute-done.7, f32[2048,768]{1,0:T(8,128)} %copy-done.6, s32[]{:T(128)S(6)} %select_n.111), kind=kLoop, calls=%fused_computation.31 | loop fusion | flops 1572864 | bytes 7864324 | tf_op jit(solution)/shard_map/broadcast_in_dim | solution.py:164
  275.1 21.4 %reduce-scatter.2.cloned.1.call-done = bf16[128,2048]{1,0:T(8,128)(2,1)} async-done(((bf16[1024,2048]{1,0:T(8,128)(2,1)}), bf16[128,2048]{1,0:T(8,128)(2,1)}) %reduce-scatter.2.cloned.1.call-update) | async-done | bytes 524304 | tf_op jit(solution)/shard_map/reduce_scatter | solution.py:153
  (60 shorter events, 0.6 us)
Async XLA Ops:
  7.2 164.8 %copy-start = (bf16[1,2048,768]{2,1,0:T(8,128)(2,1)S(1)}, bf16[1,2048,768]{2,1,0:T(8,128)(2,1)}, u32[]{:S(2)}) copy-start(bf16[1,2048,768]{2,1,0:T(8,128)(2,1)} %param.10) | copy-start | bytes 9437188
  7.2 15.0 %copy-start.9 = (s32[128,4]{0,1:T(4,128)S(1)}, s32[128,4]{0,1:T(4,128)}, u32[]{:S(2)}) copy-start(s32[128,4]{0,1:T(4,128)} %param.8) | copy-start | bytes 6148
  7.2 15.0 %copy-start.10 = (f32[128,4]{0,1:T(4,128)S(1)}, f32[128,4]{0,1:T(4,128)}, u32[]{:S(2)}) copy-start(f32[128,4]{0,1:T(4,128)} %param.9) | copy-start | bytes 6148
  7.2 61.6 %all-gather.5.cloned.1.call-start = ((), (), s32[]{:S(2)}) async-start(), calls=%async_computation.6 | async-start | bytes 4718592 | tf_op jit(solution)/shard_map/all_gather | solution.py:108
  12.7 38.4 %all-to-all-start = ((bf16[16,56,512]{2,1,0:T(8,128)(2,1)}), bf16[16,56,512]{2,1,0:T(8,128)(2,1)}, u32[]{:S(2)}, u32[]{:S(2)}) async-start(bf16[16,56,512]{2,1,0:T(8,128)(2,1)} %bitcast.69), calls=%async_computation | async-start | bytes 1835008 | tf_op jit(solution)/shard_map/all_to_all | solution.py:111
  20.4 94.2 %all-gather.3.cloned.1.call-start = ((), (), s32[]{:S(2)}) async-start(), calls=%async_computation.5 | async-start | bytes 3538944 | tf_op jit(solution)/shard_map/all_gather | solution.py:108
  77.3 55.8 %all-to-all-start.1 = ((bf16[16,56,2048]{2,1,0:T(8,128)(2,1)}), bf16[16,56,2048]{2,1,0:T(8,128)(2,1)}, u32[]{:S(2)}, u32[]{:S(2)}) async-start(bf16[16,56,2048]{2,1,0:T(8,128)(2,1)} %bitcast.66), calls=%async_computation.1 | async-start | bytes 7340032 | tf_op jit(solution)/shard_map/all_to_all | solution.py:111
  116.6 10.3 %collective-permute-start.1 = (bf16[112,512]{1,0:T(8,128)(2,1)S(1)}, bf16[112,512]{1,0:T(8,128)(2,1)S(1)}, u32[]{:S(2)}, u32[]{:S(2)}) collective-permute-start(bf16[112,512]{1,0:T(8,128)(2,1)S(1)} %get-tuple-element.34), channel_id=1, source_target_pairs={{0,32},{16,48},{32,64},{48,80},{64,96},{80,112},{96,0},{112,16},{1... | collective-permute-start | bytes 344072 | tf_op jit(solution)/shard_map/ppermute | solution.py:118
  118.2 8.7 %collective-permute-start = (bf16[112,512]{1,0:T(8,128)(2,1)S(1)}, bf16[112,512]{1,0:T(8,128)(2,1)S(1)}, u32[]{:S(2)}, u32[]{:S(2)}) collective-permute-start(bf16[112,512]{1,0:T(8,128)(2,1)S(1)} %get-tuple-element.35), channel_id=1, source_target_pairs={{0,16},{16,32},{32,48},{48,64},{64,80},{80,96},{96,112},{112,0},{1... | collective-permute-start | bytes 344072 | tf_op jit(solution)/shard_map/ppermute | solution.py:118
  133.0 46.0 %all-to-all-start.2 = ((bf16[16,56,1536]{2,1,0:T(8,128)(2,1)}), bf16[16,56,1536]{2,1,0:T(8,128)(2,1)}, u32[]{:S(2)}, u32[]{:S(2)}) async-start(bf16[16,56,1536]{2,1,0:T(8,128)(2,1)} %bitcast.70), calls=%async_computation.2 | async-start | bytes 5505024 | tf_op jit(solution)/shard_map/all_to_all | solution.py:111
  144.8 151.7 %reduce-scatter.2.cloned.1.call-start = ((), (), s32[]{:S(2)}) async-start(), calls=%async_computation.7 | async-start | bytes 4718592 | tf_op jit(solution)/shard_map/reduce_scatter | solution.py:153
  144.8 8.5 %collective-permute-start.6 = (bf16[112,512]{1,0:T(8,128)(2,1)}, bf16[112,512]{1,0:T(8,128)(2,1)S(1)}, u32[]{:S(2)}, u32[]{:S(2)}) collective-permute-start(bf16[112,512]{1,0:T(8,128)(2,1)} %get-tuple-element.29), channel_id=1, source_target_pairs={{0,112},{16,0},{32,16},{48,32},{64,48},{80,64},{96,80},{112,96},{1... | collective-permute-start | bytes 344072 | tf_op jit(solution)/shard_map/ppermute | solution.py:118
  146.1 8.7 %collective-permute-start.5 = (bf16[112,512]{1,0:T(8,128)(2,1)}, bf16[112,512]{1,0:T(8,128)(2,1)S(1)}, u32[]{:S(2)}, u32[]{:S(2)}) collective-permute-start(bf16[112,512]{1,0:T(8,128)(2,1)} %get-tuple-element.30), channel_id=1, source_target_pairs={{0,96},{16,112},{32,0},{48,16},{64,32},{80,48},{96,64},{112,80},{1... | collective-permute-start | bytes 344072 | tf_op jit(solution)/shard_map/ppermute | solution.py:118
  148.0 9.3 %collective-permute-start.4 = (bf16[112,512]{1,0:T(8,128)(2,1)}, bf16[112,512]{1,0:T(8,128)(2,1)S(1)}, u32[]{:S(2)}, u32[]{:S(2)}) collective-permute-start(bf16[112,512]{1,0:T(8,128)(2,1)} %get-tuple-element.31), channel_id=1, source_target_pairs={{0,80},{16,96},{32,112},{48,0},{64,16},{80,32},{96,48},{112,64},{1... | collective-permute-start | bytes 344072 | tf_op jit(solution)/shard_map/ppermute | solution.py:118
  150.1 9.4 %collective-permute-start.3 = (bf16[112,512]{1,0:T(8,128)(2,1)}, bf16[112,512]{1,0:T(8,128)(2,1)S(1)}, u32[]{:S(2)}, u32[]{:S(2)}) collective-permute-start(bf16[112,512]{1,0:T(8,128)(2,1)} %get-tuple-element.32), channel_id=1, source_target_pairs={{0,64},{16,80},{32,96},{48,112},{64,0},{80,16},{96,32},{112,48},{1... | collective-permute-start | bytes 344072 | tf_op jit(solution)/shard_map/ppermute | solution.py:118
  152.5 16.0 %collective-permute-start.2 = (bf16[112,512]{1,0:T(8,128)(2,1)}, bf16[112,512]{1,0:T(8,128)(2,1)S(1)}, u32[]{:S(2)}, u32[]{:S(2)}) collective-permute-start(bf16[112,512]{1,0:T(8,128)(2,1)} %get-tuple-element.33), channel_id=1, source_target_pairs={{0,48},{16,64},{32,80},{48,96},{64,112},{80,0},{96,16},{112,32},{1... | collective-permute-start | bytes 344072 | tf_op jit(solution)/shard_map/ppermute | solution.py:118
  168.5 1.4 copy-start.2
  171.1 0.9 copy-start.3
  179.1 3.7 %copy-start.4 = (bf16[896,512]{1,0:T(8,128)(2,1)S(1)}, bf16[896,512]{1,0:T(8,128)(2,1)}, u32[]{:S(2)}) copy-start(bf16[896,512]{1,0:T(8,128)(2,1)} %copy-done.3) | copy-start | bytes 2752516
  179.1 3.7 %copy-start.11 = (f32[896,768]{0,1:T(8,128)S(1)}, f32[896,768]{0,1:T(8,128)}, u32[]{:S(2)}) copy-start(f32[896,768]{0,1:T(8,128)} %fusion.14) | copy-start | bytes 8257540
  184.7 3.4 %copy-start.13 = (bf16[896,384]{0,1:T(8,128)(2,1)}, bf16[896,384]{0,1:T(8,128)(2,1)S(1)}, u32[]{:S(2)}) copy-start(bf16[896,384]{0,1:T(8,128)(2,1)S(1)} %get-tuple-element.27) | copy-start | bytes 2064388
  184.7 3.4 %copy-start.15 = (bf16[896,384]{0,1:T(8,128)(2,1)}, bf16[896,384]{0,1:T(8,128)(2,1)S(1)}, u32[]{:S(2)}) copy-start(bf16[896,384]{0,1:T(8,128)(2,1)S(1)} %get-tuple-element.28) | copy-start | bytes 2064388
  188.1 49.7 %copy-start.8 = (bf16[896,1024]{1,0:T(8,128)(2,1)S(1)}, bf16[896,1024]{1,0:T(8,128)(2,1)}, u32[]{:S(2)}) copy-start(bf16[896,1024]{1,0:T(8,128)(2,1)} %fusion.4) | copy-start | bytes 5505028
  244.0 1.1 copy-start.14
  244.0 1.3 copy-start.16
  250.9 4.4 %copy-start.6 = (f32[2048,768]{1,0:T(8,128)}, f32[2048,768]{1,0:T(8,128)S(1)}, u32[]{:S(2)}) copy-start(f32[2048,768]{1,0:T(8,128)S(1)} %fusion.20) | copy-start | bytes 18874372
  250.9 7.6 %copy-start.5 = (bf16[896,512]{1,0:T(8,128)(2,1)S(1)}, bf16[896,512]{1,0:T(8,128)(2,1)}, u32[]{:S(2)}) copy-start(bf16[896,512]{1,0:T(8,128)(2,1)} %copy-done.3) | copy-start | bytes 2752516
  250.9 7.6 %copy-start.12 = (f32[896,768]{0,1:T(8,128)S(1)}, f32[896,768]{0,1:T(8,128)}, u32[]{:S(2)}) copy-start(f32[896,768]{0,1:T(8,128)} %fusion.14) | copy-start | bytes 8257540
  255.3 15.4 %collective-permute-start.7 = (f32[1024,768]{1,0:T(8,128)}, f32[1024,768]{1,0:T(8,128)}, u32[]{:S(2)}, u32[]{:S(2)}) collective-permute-start(f32[1024,768]{1,0:T(8,128)} %constant_dynamic-slice_fusion.1), channel_id=1, source_target_pairs={{0,128},{128,0},{1,129},{129,1},{2,130},{130,2},{3,131},{131,3},{4... | collective-permute-start | bytes 9437192 | tf_op jit(solution)/shard_map/ppermute | solution.py:163
  262.1 1.6 copy-start.7
  263.9 3.6 %collective-permute-start.8 = (f32[384,1024]{1,0:T(8,128)S(1)}, f32[384,1024]{1,0:T(8,128)}, u32[]{:S(2)}, u32[]{:S(2)}) collective-permute-start(f32[384,1024]{1,0:T(8,128)S(1)} %constant_dynamic-slice_fusion), channel_id=1, source_target_pairs={{0,128},{128,0},{1,129},{129,1},{2,130},{130,2},{3,131},{131,3},{4... | collective-permute-start | bytes 4718600 | tf_op jit(solution)/shard_map/ppermute | solution.py:163
  267.6 29.0 %copy-start.1 = (bf16[1,2048,768]{2,1,0:T(8,128)(2,1)S(1)}, bf16[1,2048,768]{2,1,0:T(8,128)(2,1)}, u32[]{:S(2)}) copy-start(bf16[1,2048,768]{2,1,0:T(8,128)(2,1)} %param.10) | copy-start | bytes 9437188
Sparse Core Ops, SparseCore 0:
  9.8 58.9 all-gather.4
  71.1 43.3 all-gather.2
  244.1 52.3 reduce-scatter.1

commit v3 on v2

--- a/solution.py
+++ b/solution.py
@@ -10,7 +10,8 @@
 PLANE = X * Y
 CAP = 7
 SLOTS = PLANE * CAP * Z
-GRAD_FIRST = 512
+IN_FIRST = 384
+GRAD_FIRST = 384
 
 f32 = jnp.float32
 bf16 = jnp.bfloat16
@@ -94,7 +95,7 @@
 
 
 def weave(received, parts):
-    return times("weave", received, parts, 512)
+    return times("weave", received, parts, 384)
 
 
 def body(tokens, out_grad, expert_ids, gate_weights, w_in, w_out):
@@ -123,8 +124,10 @@
     own_slots, own_gate = lax.optimization_barrier(column_slots(ids, gates))
     to_send, received = lax.optimization_barrier(order_matrices(plane))
 
-    tokens_all = gather_z(tokens)
-    first = (mm(own_slots, out_grad[:, :GRAD_FIRST], 1, 0) * own_gate).astype(bf16)
+    tokens_all = gather_z(tokens[:, IN_FIRST:])
+    first_in = mm(own_slots, tokens[:, :IN_FIRST], 1, 0).astype(bf16)
+    first_grad = (mm(own_slots, out_grad[:, :GRAD_FIRST], 1, 0) * own_gate).astype(bf16)
+    first = jnp.concatenate([first_in, first_grad], axis=1)
     meta = jnp.concatenate([ids.astype(f32), gates], axis=0)
     meta, rest = lax.optimization_barrier((meta, out_grad[:, GRAD_FIRST:], first))[:2]
     first = swap_plane(first)
@@ -134,15 +137,17 @@
     meta, first = lax.optimization_barrier((meta, first))
     slots, slot_gate = lax.optimization_barrier(plane_slots(meta, plane))
     first = swap_z(lax.optimization_barrier((first, grads_all))[0])
-    rows_in = mm(slots, tokens_all, 1, 0).astype(bf16)
-    rows_in = swap_plane(rows_in)
+    rows_in = swap_plane(mm(slots, tokens_all, 1, 0).astype(bf16))
     second = (mm(slots, grads_all, 1, 0) * slot_gate).astype(bf16)
     second = lax.optimization_barrier((second, first[1], first[2], rows_in))[0]
     second = swap_plane(second)
+    joined = mm(rows_in, w_in[IN_FIRST:], 1, 0)
+    first, joined = lax.optimization_barrier((first, joined))
     first = weave(received, first)
+    first_in, first_grad = first[:, :IN_FIRST], first[:, IN_FIRST:]
 
-    joined = mm(rows_in, w_in, 1, 0)
-    d_hidden = mm(first, w_out[:, :GRAD_FIRST], 1, 1) + mm(second, w_out[:, GRAD_FIRST:], 1, 1)
+    joined = joined + mm(first_in, w_in[:IN_FIRST], 1, 0)
+    d_hidden = mm(first_grad, w_out[:, :GRAD_FIRST], 1, 1) + mm(second, w_out[:, GRAD_FIRST:], 1, 1)
     gate_part, up_part = joined[:, :half], joined[:, half:]
     activated, derivative = silu_parts(gate_part)
     hidden = (activated * up_part).astype(bf16)
@@ -152,8 +157,8 @@
     part = mm(slots, back, 0, 0).astype(bf16)
     token_grad = lax.psum_scatter(part, "z", scatter_dimension=0, tiled=True)
 
-    grad_in = mm(rows_in, d_joined, 0, 0)
-    grad_out = mm(hidden, jnp.concatenate([first, second], axis=1), 0, 0)
+    grad_in = mm(jnp.concatenate([first_in, rows_in], axis=1), d_joined, 0, 0)
+    grad_out = mm(hidden, jnp.concatenate([first_grad, second], axis=1), 0, 0)
     half_width = width // 2
     other = 1 - core
 

time: 304 us -> 299 us (0.984)
  blocking collectives: 73.9 us -> 70.6 us
    reduce_scatter x1, waiting for transfers between devices: 21.4 us -> 29.9 us  [body(): token_grad = lax.psum_scatter(part, 'z', scatter_dimension=0, tiled=True)]
    all_to_all x3, waiting for transfers between devices: 6.15 us -> 0.01 us  [swap_plane(): lax.all_to_all(x, ('x', 'y'), split_axis=0, concat_axis=0, tiled=True)]
    all_to_all x3, starting transfers between devices: 26 us -> 21 us  [swap_plane(): lax.all_to_all(x, ('x', 'y'), split_axis=0, concat_axis=0, tiled=True)]
    all_to_all x1, blocking collectives: 49.6 us -> 46.3 us  [swap_plane(): lax.all_to_all(x, ('x', 'y'), split_axis=0, concat_axis=0, tiled=True)]
    ppermute x2, starting transfers between devices: 3.64 us -> 7 us  [sum_cores(): got = lax.ppermute(send, 'dp', [(0, 1), (1, 0)])]
    dot_general x13 -> x15, matrix products: 53.3 us -> 51.1 us  [mm(): lax.dot_general(a, b, (((ca,), (cb,)), ((), ())), preferred_element_type=...]
    unnamed x36 -> x44, local copies, waits for them, and re-layouts: 7.94 us -> 6.57 us
  transfers between devices with their start and end apart: 15 -> 15, of which waited for: 9 -> 7; matrix products, arithmetic and copies ran while one was open for 20% -> 19% of each run, Pallas kernels for 0% -> 1%
where the time goes in v3:
time: 299 us
  waiting for transfers between devices  90.9 us (30%)
  blocking collectives  70.6 us (24%)
  matrix products  51.1 us (17%)
  starting transfers between devices  41.2 us (14%)
  other arithmetic  14.5 us (5%)
  between operations  14.2 us (5%)
  local copies, waits for them, and re-layouts  13.8 us (5%)
    dot_general x15, matrix products, mm(): lax.dot_general(a, b, (((ca,), (cb,)), ((), ())), preferred_element_type=...  51.1 us
    all_to_all x1, blocking collectives, swap_plane(): lax.all_to_all(x, ('x', 'y'), split_axis=0, concat_axis=0, tiled=True)  46.3 us
    all_gather x2, waiting for transfers between devices, gather_z(): return lax.all_gather(x, 'z', axis=0, tiled=True)  41.4 us
    reduce_scatter x1, waiting for transfers between devices, body(): token_grad = lax.psum_scatter(part, 'z', scatter_dimension=0, tiled=True)  29.9 us
    all_gather x1, blocking collectives, gather_z(): return lax.all_gather(x, 'z', axis=0, tiled=True)  24.3 us
    all_to_all x3, starting transfers between devices, swap_plane(): lax.all_to_all(x, ('x', 'y'), split_axis=0, concat_axis=0, tiled=True)  21 us
    ppermute x7, waiting for transfers between devices, swap_z(): lax.ppermute(piece, 'z', [(i, (i + distance) % Z) for i in range(Z)])  16.1 us
    ppermute x7, starting transfers between devices, swap_z(): lax.ppermute(piece, 'z', [(i, (i + distance) % Z) for i in range(Z)])  13.1 us
  transfers between devices with their start and end apart: 15, of which 7 were waited for; matrix products, arithmetic and copies ran while one was open for 19% of the time, Pallas kernels for 1%

profile of v3, /device:TPU:1, one launch (start us, length us, event | category | flops | bytes accessed | tf_op | source)
XLA Modules:
  0.0 298.7 jit_solution(12234828581629089055)
XLA Ops:
  7.2 1.8 slice.85
  9.1 0.7 fusion.33
  9.8 0.1 convolution_select_fusion.1
  10.2 0.7 select_reduce_fusion.2
  10.9 0.3 select_reduce_fusion.1
  11.2 0.1 reshape.109
  11.3 0.2 fusion.30
  11.5 1.3 convolution_convert_fusion.4
  12.8 0.4 fusion.23
  13.2 0.1 pad_maximum_fusion
  13.4 1.5 copy.24
  14.9 7.6 %all-to-all-start = ((bf16[16,56,768]{2,1,0:T(8,128)(2,1)}), bf16[16,56,768]{2,1,0:T(8,128)(2,1)}, u32[]{:S(2)}, u32[]{:S(2)}) async-start(bf16[16,56,768]{2,1,0:T(8,128)(2,1)} %bitcast.7), calls=%async_computation | async-start | bytes 2752512 | tf_op jit(solution)/shard_map/all_to_all | solution.py:112
  22.6 0.8 slice.72
  23.6 2.2 fusion.15
  25.8 24.3 %all_gather.9 = f32[64,128]{1,0:T(8,128)S(1)} all-gather(f32[8,128]{1,0:T(8,128)S(1)} %pad_maximum_fusion.4), channel_id=1, replica_groups=mesh['dp'=2,'z'=8,'x'=4,'y'=4] {'z'}, dimensions={0}, use_global_device_ids=true | all-gather | bytes 36864 | tf_op jit(solution)/shard_map/all_gather | solution.py:109
  50.1 4.0 %convolution_convert_fusion.3 = bf16[896,768]{1,0:T(8,128)(2,1)} fusion(bf16[896,896]{1,0:T(8,128)(2,1)S(1)} %get-tuple-element.27, bf16[896,768]{1,0:T(8,128)(2,1)} %bitcast.8), kind=kOutput, calls=%fused_computation.35 | convolution fusion | flops 1233813504 | bytes 4358144 | tf_op jit(solution)/shard_map/dot_general | solution.py:21
  54.2 0.1 fusion.32
  54.3 0.1 compare_reduce_fusion
  54.4 0.1 convolution_select_fusion
  54.6 0.3 select_reduce_fusion
  54.8 0.1 reshape.111
  55.0 0.4 fusion.8
  55.4 6.6 %all-gather.5.cloned.1.call-done = bf16[1024,1664]{1,0:T(8,128)(2,1)} async-done(((bf16[128,1664]{1,0:T(8,128)(2,1)}), bf16[1024,1664]{1,0:T(8,128)(2,1)}) %all-gather.5.cloned.1.call-update) | async-done | bytes 3407888 | tf_op jit(solution)/shard_map/all_gather | solution.py:109
  62.0 6.8 %convolution_convert_fusion.2 = bf16[896,1664]{1,0:T(8,128)(2,1)} fusion(bf16[896,1024]{1,0:T(8,128)(2,1)S(1)} %fusion.8, bf16[1024,1664]{1,0:T(8,128)(2,1)} %all-gather.5.cloned.1.call-done), kind=kOutput, calls=%fused_computation.19 | convolution fusion | flops 3054944256 | bytes 8224768 | tf_op jit(solution)/shard_map/dot_general | solution.py:21
  68.8 6.7 %all-to-all-start.1 = ((bf16[16,56,1664]{2,1,0:T(8,128)(2,1)}), bf16[16,56,1664]{2,1,0:T(8,128)(2,1)}, u32[]{:S(2)}, u32[]{:S(2)}) async-start(bf16[16,56,1664]{2,1,0:T(8,128)(2,1)} %bitcast.72), calls=%async_computation.1 | async-start | bytes 5963776 | tf_op jit(solution)/shard_map/all_to_all | solution.py:112
  75.5 34.9 %all-gather.3.cloned.1.call-done = bf16[1024,1664]{1,0:T(8,128)(2,1)} async-done(((bf16[128,1664]{1,0:T(8,128)(2,1)}), bf16[1024,1664]{1,0:T(8,128)(2,1)}) %all-gather.3.cloned.1.call-update) | async-done | bytes 3407888 | tf_op jit(solution)/shard_map/all_gather | solution.py:109
  110.4 0.9 fusion.57
  111.3 1.0 collective-permute-start.1
  112.3 2.0 collective-permute-start
  114.3 7.6 %multiply_convert_fusion = bf16[896,1664]{1,0:T(8,128)(2,1)} fusion(bf16[896,1024]{1,0:T(8,128)(2,1)} %copy-done.4, bf16[1024,1664]{1,0:T(8,128)(2,1)} %all-gather.3.cloned.1.call-done, f32[896]{0:T(1024)S(1)} %reduce.3), kind=kOutput, calls=%fused_computation | convolution fusion | flops 3056435200 | bytes 8228352 | tf_op jit(solution)/shard_map/dot_general | solution.py:21
  121.9 1.5 collective-permute-done.refs_1_
  123.5 6.7 %all-to-all-start.2 = ((bf16[16,56,1664]{2,1,0:T(8,128)(2,1)}), bf16[16,56,1664]{2,1,0:T(8,128)(2,1)}, u32[]{:S(2)}, u32[]{:S(2)}) async-start(bf16[16,56,1664]{2,1,0:T(8,128)(2,1)} %bitcast.71), calls=%async_computation.2 | async-start | bytes 5963776 | tf_op jit(solution)/shard_map/all_to_all | solution.py:112
  130.3 3.3 %collective-permute-start.6 = (bf16[112,768]{1,0:T(8,128)(2,1)S(1)}, bf16[112,768]{1,0:T(8,128)(2,1)S(1)}, u32[]{:S(2)}, u32[]{:S(2)}) collective-permute-start(bf16[112,768]{1,0:T(8,128)(2,1)S(1)} %copy-done.12), channel_id=1, source_target_pairs={{0,112},{16,0},{32,16},{48,32},{64,48},{80,64},{96,80},{112,96},{1... | collective-permute-start | bytes 516104 | tf_op jit(solution)/shard_map/ppermute | solution.py:119
  133.5 0.6 collective-permute-start.5
  134.2 2.9 collective-permute-start.4
  137.1 1.9 collective-permute-start.3
  139.0 1.4 collective-permute-start.2
  140.4 5.3 %fusion.18 = f32[896,768]{1,0:T(8,128)S(1)} fusion(bf16[896,1664]{1,0:T(8,128)(2,1)} %bitcast.15, bf16[1,2048,768]{2,1,0:T(8,128)(2,1)} %param.10), kind=kOutput, calls=%fused_computation.32 | convolution fusion | flops 2290089984 | bytes 8290304 | tf_op jit(solution)/shard_map/dot_general | solution.py:21
  145.7 8.9 %collective-permute-done.4.refs_5_ = bf16[112,768]{1,0:T(8,128)(2,1)S(1)} collective-permute-done((bf16[112,768]{1,0:T(8,128)(2,1)S(1)}, bf16[112,768]{1,0:T(8,128)(2,1)S(1)}, u32[]{:S(2)}, u32[]{:S(2)}) %collective-permute-start.4) | collective-permute-done | bytes 172064 | tf_op jit(solution)/shard_map/ppermute | solution.py:119
  154.6 5.6 %collective-permute-done.2.refs_3_ = bf16[112,768]{1,0:T(8,128)(2,1)S(1)} collective-permute-done((bf16[112,768]{1,0:T(8,128)(2,1)S(1)}, bf16[112,768]{1,0:T(8,128)(2,1)S(1)}, u32[]{:S(2)}, u32[]{:S(2)}) %collective-permute-start.2) | collective-permute-done | bytes 172064 | tf_op jit(solution)/shard_map/ppermute | solution.py:119
  160.3 2.4 weave.1
  162.7 1.9 fusion.27
  164.6 1.9 add.95
  166.5 3.8 %fusion.24 = f32[896,384]{1,0:T(8,128)S(1)} fusion(bf16[896,1664]{1,0:T(8,128)(2,1)} %bitcast.19, bf16[384,2048]{1,0:T(8,128)(2,1)S(1)} %bitcast.83), kind=kOutput, calls=%fused_computation.49 | convolution fusion | flops 1145044992 | bytes 5636096 | tf_op jit(solution)/shard_map/dot_general | solution.py:21
  170.3 1.0 multiply_convert_fusion.3
  171.4 0.8 copy-done.13
  172.2 3.3 %convolution_convert_fusion.1 = bf16[896,2048]{1,0:T(8,128)(2,1)S(1)} fusion(bf16[1,2048,768]{2,1,0:T(8,128)(2,1)S(1)} %copy-done.13, bf16[896,384]{1,0:T(8,128)(2,1)S(1)} %get-tuple-element.46, bf16[896,384]{1,0:T(8,128)(2,1)S(1)} %get-tuple-element.45), kind=kOutput, calls=%fused_computation.18 | convolution fusion | flops 2823159808 | bytes 8192000 | tf_op jit(solution)/shard_map/dot_general | solution.py:21
  175.5 46.3 %all_to_all.48 = bf16[16,56,2048]{2,1,0:T(8,128)(2,1)S(1)} all-to-all(bf16[16,56,2048]{2,1,0:T(8,128)(2,1)S(1)} %bitcast.70), channel_id=1, replica_groups=mesh['dp'=2,'z'=8,'x'=4,'y'=4] {'x','y'}, dimensions={0} | all-to-all | bytes 7340032 | tf_op jit(solution)/shard_map/all_to_all | solution.py:112
  221.8 6.3 %convolution_convert_fusion = bf16[1024,2048]{1,0:T(8,128)(2,1)} fusion(bf16[896,1024]{1,0:T(8,128)(2,1)S(1)} %copy-done.5, bf16[896,2048]{1,0:T(8,128)(2,1)S(1)} %bitcast.69), kind=kOutput, calls=%fused_computation.7 | convolution fusion | flops 3760193536 | bytes 9699328 | tf_op jit(solution)/shard_map/dot_general | solution.py:21
  228.1 0.1 fusion.56
  228.3 0.9 copy-done.18
  229.2 0.2 copy-done.20
  229.4 5.4 %fusion = f32[2048,768]{1,0:T(8,128)S(1)} fusion(bf16[896,1664]{1,0:T(8,128)(2,1)} %bitcast.15, bf16[896,384]{1,0:T(8,128)(2,1)S(1)} %get-tuple-element.48, bf16[896,384]{1,0:T(8,128)(2,1)S(1)} %copy-done.20, bf16[896,384]{1,0:T(8,128)(2,1)S(1)} %copy-done.18), kind=kOutput, calls=%fused_computation.8 | convolution fusion | flops 2828664832 | bytes 11337728 | tf_op jit(solution)/shard_map/dot_general | solution.py:21
  234.8 0.2 constant_dynamic-slice_fusion.1
  235.0 2.9 copy-done
  237.9 6.2 %collective-permute-start.7 = (f32[1024,768]{1,0:T(8,128)S(1)}, f32[1024,768]{1,0:T(8,128)}, u32[]{:S(2)}, u32[]{:S(2)}) collective-permute-start(f32[1024,768]{1,0:T(8,128)S(1)} %constant_dynamic-slice_fusion.1), channel_id=1, source_target_pairs={{0,128},{128,0},{1,129},{129,1},{2,130},{130,2},{3,131},{131,3},{4... | collective-permute-start | bytes 9437192 | tf_op jit(solution)/shard_map/ppermute | solution.py:168
  244.1 3.7 %fusion.4 = f32[384,2048]{1,0:T(8,128)S(1)} fusion(bf16[896,1664]{1,0:T(8,128)(2,1)} %bitcast.19, bf16[896,384]{1,0:T(8,128)(2,1)S(1)} %get-tuple-element.47, f32[896,768]{1,0:T(8,128)S(1)} %copy-done.3), kind=kOutput, calls=%fused_computation.12 | convolution fusion | flops 1418690560 | bytes 9568256 | tf_op jit(solution)/shard_map/dot_general | solution.py:21
  247.8 1.6 copy-done.1
  249.5 1.3 constant_dynamic-slice_fusion
  250.8 0.8 collective-permute-start.8
  251.5 3.4 %collective-permute-done.8 = f32[384,1024]{1,0:T(8,128)} collective-permute-done((f32[384,1024]{1,0:T(8,128)}, f32[384,1024]{1,0:T(8,128)}, u32[]{:S(2)}, u32[]{:S(2)}) %collective-permute-start.8) | collective-permute-done | bytes 1572896 | tf_op jit(solution)/shard_map/ppermute | solution.py:168
  254.9 3.0 %fusion.26 = bf16[1,384,1024]{2,1,0:T(8,128)(2,1)} fusion(f32[384,1024]{1,0:T(8,128)} %collective-permute-done.8, f32[384,2048]{1,0:T(8,128)} %copy-done.1, s32[]{:T(128)S(6)} %select_n.111), kind=kLoop, calls=%fused_computation.53 | loop fusion | flops 786432 | bytes 3932164 | tf_op jit(solution)/shard_map/broadcast_in_dim | solution.py:169
  257.9 4.4 %fusion.21 = bf16[1,1024,768]{2,1,0:T(8,128)(2,1)} fusion(f32[1024,768]{1,0:T(8,128)} %collective-permute-done.7, f32[2048,768]{1,0:T(8,128)} %copy-done, s32[]{:T(128)S(6)} %select_n.111), kind=kLoop, calls=%fused_computation.36 | loop fusion | flops 1572864 | bytes 7864324 | tf_op jit(solution)/shard_map/broadcast_in_dim | solution.py:169
  262.3 29.9 %reduce-scatter.2.cloned.1.call-done = bf16[128,2048]{1,0:T(8,128)(2,1)} async-done(((bf16[1024,2048]{1,0:T(8,128)(2,1)}), bf16[128,2048]{1,0:T(8,128)(2,1)}) %reduce-scatter.2.cloned.1.call-update) | async-done | bytes 524304 | tf_op jit(solution)/shard_map/reduce_scatter | solution.py:158
  (75 shorter events, 0.8 us)
Async XLA Ops:
  7.2 5.7 %copy-start.7 = (bf16[128,2048]{1,0:T(8,128)(2,1)S(1)}, bf16[128,2048]{1,0:T(8,128)(2,1)}, u32[]{:S(2)}) copy-start(bf16[128,2048]{1,0:T(8,128)(2,1)} %param.7) | copy-start | bytes 1572868
  7.2 54.8 %all-gather.5.cloned.1.call-start = ((), (), s32[]{:S(2)}) async-start(), calls=%async_computation.6 | async-start | bytes 3833856 | tf_op jit(solution)/shard_map/all_gather | solution.py:109
  13.4 10.0 %copy-start.14 = (s32[128,4]{0,1:T(4,128)S(1)}, s32[128,4]{0,1:T(4,128)}, u32[]{:S(2)}) copy-start(s32[128,4]{0,1:T(4,128)} %param.8) | copy-start | bytes 6148
  13.4 10.0 %copy-start.15 = (f32[128,4]{0,1:T(4,128)S(1)}, f32[128,4]{0,1:T(4,128)}, u32[]{:S(2)}) copy-start(f32[128,4]{0,1:T(4,128)} %param.9) | copy-start | bytes 6148
  14.9 35.2 %all-to-all-start = ((bf16[16,56,768]{2,1,0:T(8,128)(2,1)}), bf16[16,56,768]{2,1,0:T(8,128)(2,1)}, u32[]{:S(2)}, u32[]{:S(2)}) async-start(bf16[16,56,768]{2,1,0:T(8,128)(2,1)} %bitcast.7), calls=%async_computation | async-start | bytes 2752512 | tf_op jit(solution)/shard_map/all_to_all | solution.py:112
  22.6 87.8 %all-gather.3.cloned.1.call-start = ((), (), s32[]{:S(2)}) async-start(), calls=%async_computation.5 | async-start | bytes 3833856 | tf_op jit(solution)/shard_map/all_gather | solution.py:109
  55.4 13.4 %copy-start.4 = (bf16[896,1024]{1,0:T(8,128)(2,1)}, bf16[896,1024]{1,0:T(8,128)(2,1)S(1)}, u32[]{:S(2)}) copy-start(bf16[896,1024]{1,0:T(8,128)(2,1)S(1)} %fusion.8) | copy-start | bytes 5505028
  68.8 41.6 %copy-start.6 = (bf16[896,768]{1,0:T(8,128)(2,1)S(1)}, bf16[896,768]{1,0:T(8,128)(2,1)}, u32[]{:S(2)}) copy-start(bf16[896,768]{1,0:T(8,128)(2,1)} %convolution_convert_fusion.3) | copy-start | bytes 4128772
  68.8 54.7 %all-to-all-start.1 = ((bf16[16,56,1664]{2,1,0:T(8,128)(2,1)}), bf16[16,56,1664]{2,1,0:T(8,128)(2,1)}, u32[]{:S(2)}, u32[]{:S(2)}) async-start(bf16[16,56,1664]{2,1,0:T(8,128)(2,1)} %bitcast.72), calls=%async_computation.1 | async-start | bytes 5963776 | tf_op jit(solution)/shard_map/all_to_all | solution.py:112
  111.3 10.6 %collective-permute-start.1 = (bf16[112,768]{1,0:T(8,128)(2,1)S(1)}, bf16[112,768]{1,0:T(8,128)(2,1)S(1)}, u32[]{:S(2)}, u32[]{:S(2)}) collective-permute-start(bf16[112,768]{1,0:T(8,128)(2,1)S(1)} %get-tuple-element.54), channel_id=1, source_target_pairs={{0,32},{16,48},{32,64},{48,80},{64,96},{80,112},{96,0},{112,16},{1... | collective-permute-start | bytes 516104 | tf_op jit(solution)/shard_map/ppermute | solution.py:119
  112.3 11.1 %collective-permute-start = (bf16[112,768]{1,0:T(8,128)(2,1)S(1)}, bf16[112,768]{1,0:T(8,128)(2,1)S(1)}, u32[]{:S(2)}, u32[]{:S(2)}) collective-permute-start(bf16[112,768]{1,0:T(8,128)(2,1)S(1)} %get-tuple-element.55), channel_id=1, source_target_pairs={{0,16},{16,32},{32,48},{48,64},{64,80},{80,96},{96,112},{112,0},{1... | collective-permute-start | bytes 516104 | tf_op jit(solution)/shard_map/ppermute | solution.py:119
  123.5 6.8 %copy-start.12 = (bf16[112,768]{1,0:T(8,128)(2,1)S(1)}, bf16[112,768]{1,0:T(8,128)(2,1)}, u32[]{:S(2)}) copy-start(bf16[112,768]{1,0:T(8,128)(2,1)} %get-tuple-element.49) | copy-start | bytes 516100
  123.5 10.1 %copy-start.11 = (bf16[112,768]{1,0:T(8,128)(2,1)S(1)}, bf16[112,768]{1,0:T(8,128)(2,1)}, u32[]{:S(2)}) copy-start(bf16[112,768]{1,0:T(8,128)(2,1)} %get-tuple-element.50) | copy-start | bytes 516100
  123.5 10.7 %copy-start.10 = (bf16[112,768]{1,0:T(8,128)(2,1)S(1)}, bf16[112,768]{1,0:T(8,128)(2,1)}, u32[]{:S(2)}) copy-start(bf16[112,768]{1,0:T(8,128)(2,1)} %get-tuple-element.51) | copy-start | bytes 516100
  123.5 13.6 %copy-start.9 = (bf16[112,768]{1,0:T(8,128)(2,1)S(1)}, bf16[112,768]{1,0:T(8,128)(2,1)}, u32[]{:S(2)}) copy-start(bf16[112,768]{1,0:T(8,128)(2,1)} %get-tuple-element.52) | copy-start | bytes 516100
  123.5 15.5 %copy-start.8 = (bf16[112,768]{1,0:T(8,128)(2,1)S(1)}, bf16[112,768]{1,0:T(8,128)(2,1)}, u32[]{:S(2)}) copy-start(bf16[112,768]{1,0:T(8,128)(2,1)} %get-tuple-element.53) | copy-start | bytes 516100
  123.5 43.0 %all-to-all-start.2 = ((bf16[16,56,1664]{2,1,0:T(8,128)(2,1)}), bf16[16,56,1664]{2,1,0:T(8,128)(2,1)}, u32[]{:S(2)}, u32[]{:S(2)}) async-start(bf16[16,56,1664]{2,1,0:T(8,128)(2,1)} %bitcast.71), calls=%async_computation.2 | async-start | bytes 5963776 | tf_op jit(solution)/shard_map/all_to_all | solution.py:112
  130.2 162.0 %reduce-scatter.2.cloned.1.call-start = ((), (), s32[]{:S(2)}) async-start(), calls=%async_computation.7 | async-start | bytes 4718592 | tf_op jit(solution)/shard_map/reduce_scatter | solution.py:158
  130.3 15.4 %collective-permute-start.6 = (bf16[112,768]{1,0:T(8,128)(2,1)S(1)}, bf16[112,768]{1,0:T(8,128)(2,1)S(1)}, u32[]{:S(2)}, u32[]{:S(2)}) collective-permute-start(bf16[112,768]{1,0:T(8,128)(2,1)S(1)} %copy-done.12), channel_id=1, source_target_pairs={{0,112},{16,0},{32,16},{48,32},{64,48},{80,64},{96,80},{112,96},{1... | collective-permute-start | bytes 516104 | tf_op jit(solution)/shard_map/ppermute | solution.py:119
  133.5 12.1 %collective-permute-start.5 = (bf16[112,768]{1,0:T(8,128)(2,1)S(1)}, bf16[112,768]{1,0:T(8,128)(2,1)S(1)}, u32[]{:S(2)}, u32[]{:S(2)}) collective-permute-start(bf16[112,768]{1,0:T(8,128)(2,1)S(1)} %copy-done.11), channel_id=1, source_target_pairs={{0,96},{16,112},{32,0},{48,16},{64,32},{80,48},{96,64},{112,80},{1... | collective-permute-start | bytes 516104 | tf_op jit(solution)/shard_map/ppermute | solution.py:119
  134.2 20.4 %collective-permute-start.4 = (bf16[112,768]{1,0:T(8,128)(2,1)S(1)}, bf16[112,768]{1,0:T(8,128)(2,1)S(1)}, u32[]{:S(2)}, u32[]{:S(2)}) collective-permute-start(bf16[112,768]{1,0:T(8,128)(2,1)S(1)} %copy-done.10), channel_id=1, source_target_pairs={{0,80},{16,96},{32,112},{48,0},{64,16},{80,32},{96,48},{112,64},{1... | collective-permute-start | bytes 516104 | tf_op jit(solution)/shard_map/ppermute | solution.py:119
  137.1 17.5 %collective-permute-start.3 = (bf16[112,768]{1,0:T(8,128)(2,1)S(1)}, bf16[112,768]{1,0:T(8,128)(2,1)S(1)}, u32[]{:S(2)}, u32[]{:S(2)}) collective-permute-start(bf16[112,768]{1,0:T(8,128)(2,1)S(1)} %copy-done.9), channel_id=1, source_target_pairs={{0,64},{16,80},{32,96},{48,112},{64,0},{80,16},{96,32},{112,48},{1... | collective-permute-start | bytes 516104 | tf_op jit(solution)/shard_map/ppermute | solution.py:119
  139.0 21.3 %collective-permute-start.2 = (bf16[112,768]{1,0:T(8,128)(2,1)S(1)}, bf16[112,768]{1,0:T(8,128)(2,1)S(1)}, u32[]{:S(2)}, u32[]{:S(2)}) collective-permute-start(bf16[112,768]{1,0:T(8,128)(2,1)S(1)} %copy-done.8), channel_id=1, source_target_pairs={{0,48},{16,64},{32,80},{48,96},{64,112},{80,0},{96,16},{112,32},{1... | collective-permute-start | bytes 516104 | tf_op jit(solution)/shard_map/ppermute | solution.py:119
  164.6 1.9 copy-start.16
  166.5 3.8 %copy-start.2 = (f32[896,768]{1,0:T(8,128)S(1)}, f32[896,768]{1,0:T(8,128)}, u32[]{:S(2)}) copy-start(f32[896,768]{1,0:T(8,128)} %add.95) | copy-start | bytes 8257540
  170.3 1.9 copy-start.13
  171.4 4.1 %copy-start.17 = (bf16[896,384]{1,0:T(8,128)(2,1)}, bf16[896,384]{1,0:T(8,128)(2,1)S(1)}, u32[]{:S(2)}) copy-start(bf16[896,384]{1,0:T(8,128)(2,1)S(1)} %get-tuple-element.45) | copy-start | bytes 2064388
  171.4 4.1 %copy-start.19 = (bf16[896,384]{1,0:T(8,128)(2,1)}, bf16[896,384]{1,0:T(8,128)(2,1)S(1)}, u32[]{:S(2)}) copy-start(bf16[896,384]{1,0:T(8,128)(2,1)S(1)} %get-tuple-element.46) | copy-start | bytes 2064388
  175.5 46.3 %copy-start.5 = (bf16[896,1024]{1,0:T(8,128)(2,1)S(1)}, bf16[896,1024]{1,0:T(8,128)(2,1)}, u32[]{:S(2)}) copy-start(bf16[896,1024]{1,0:T(8,128)(2,1)} %copy-done.4) | copy-start | bytes 5505028
  228.1 1.1 copy-start.18
  228.1 1.3 copy-start.20
  234.8 3.1 %copy-start = (f32[2048,768]{1,0:T(8,128)}, f32[2048,768]{1,0:T(8,128)S(1)}, u32[]{:S(2)}) copy-start(f32[2048,768]{1,0:T(8,128)S(1)} %fusion) | copy-start | bytes 18874372
  234.8 9.3 %copy-start.3 = (f32[896,768]{1,0:T(8,128)S(1)}, f32[896,768]{1,0:T(8,128)}, u32[]{:S(2)}) copy-start(f32[896,768]{1,0:T(8,128)} %add.95) | copy-start | bytes 8257540
  237.9 20.1 %collective-permute-start.7 = (f32[1024,768]{1,0:T(8,128)S(1)}, f32[1024,768]{1,0:T(8,128)}, u32[]{:S(2)}, u32[]{:S(2)}) collective-permute-start(f32[1024,768]{1,0:T(8,128)S(1)} %constant_dynamic-slice_fusion.1), channel_id=1, source_target_pairs={{0,128},{128,0},{1,129},{129,1},{2,130},{130,2},{3,131},{131,3},{4... | collective-permute-start | bytes 9437192 | tf_op jit(solution)/shard_map/ppermute | solution.py:168
  247.8 1.6 copy-start.1
  250.8 4.1 %collective-permute-start.8 = (f32[384,1024]{1,0:T(8,128)}, f32[384,1024]{1,0:T(8,128)}, u32[]{:S(2)}, u32[]{:S(2)}) collective-permute-start(f32[384,1024]{1,0:T(8,128)} %constant_dynamic-slice_fusion), channel_id=1, source_target_pairs={{0,128},{128,0},{1,129},{129,1},{2,130},{130,2},{3,131},{131,3},{4... | collective-permute-start | bytes 4718600 | tf_op jit(solution)/shard_map/ppermute | solution.py:168
Sparse Core Ops, SparseCore 0:
  10.4 51.5 all-gather.4
  64.3 46.0 all-gather.2
  228.2 63.9 reduce-scatter.1
